TPU v7x, 256 devices: a whole 4x4x8 slice. The times are simulated.
256 devices in a mesh: tm: 8 (over y, core), space: 32 (over x, z).
Axes of the slice: x: 4, y: 4, z: 8, core: 2. Of those that a mesh axis runs over, the one named last changes fastest.
Arguments:
- ensemble: bfloat16 [16, 64, 524288], P('tm', None, 'space'), may hold values from -6 to 6
- obs_owner: int32 [16, 4096, 1], P('tm', 'space'), may hold values from 0 to 31; in each aligned block of 128 rows (0 to 127, 128 to 255, ..., all dimensions but the last counted through in order) at most 8 rows name the same one
- obs_local: int32 [16, 4096], P('tm', 'space'), may hold values from 0 to 63
- obs_offset: int32 [16, 4096, 32], P('tm', 'space'), may hold values from 0 to 255
- obs_count: int32 [16, 4096], P('tm', 'space'), may hold values from 1 to 32
- obs_value: float32 [16, 4096, 32], P('tm', 'space'), may hold values from -12 to 12
- obs_var: float32 [16, 4096, 32], P('tm', 'space'), may hold values from 512 to 8192
- inflation: float32 [16], P('tm'), may hold values from 1.2 to 1.6
Outputs:
- smoothed: float32 [16, 64, 524288], P('tm', None, 'space')
Inputs may be any that keep to these rules, and one draw needn't show every extreme that they name: `obs_owner`: in each window, the 128 observation blocks held by one index of space name any one owner at most 8 times, a bound that some block reaches.
All inputs are finite; a program needn't handle non-finite values.
Results may differ from a plain program's by a relative error of at most 0.0003.
Values may be sent and summed in bfloat16 or wider, within the bound.
No kernel may reach another device: no remote copies, remote signals or barrier semaphores. Data moves between devices by JAX's collectives and lax.ppermute only.
A program may use at most 64 MiB of HBM per device.

v0:
```python
import math

import jax
import jax.numpy as jnp
from jax import lax
from jax.sharding import PartitionSpec as P

BLOCK = 256


exact_mode = lax.Precision.HIGHEST


def carried_in(part, axis, combine, identity):
    count = lax.axis_size(axis)
    place = lax.axis_index(axis)
    ahead = count - 1 - place
    gathered = lax.all_gather(part, axis)
    state = jnp.zeros_like(part) + jnp.asarray(identity, part.dtype)

    def one(step, state):
        source = count - 1 - step
        return combine(state, lax.dynamic_index_in_dim(gathered, source, 0, False))

    return lax.fori_loop(0, ahead, one, state)


def build_transform(gram_sum, projection, inflation):
    members = gram_sum.shape[-1]
    identity = jnp.eye(members, dtype=jnp.float32)
    system = (members - 1.0) * identity + gram_sum
    factor = jnp.linalg.cholesky(system)
    mean_weight = jax.scipy.linalg.cho_solve((factor, True), projection[..., None])
    inverse = jax.scipy.linalg.solve_triangular(
        factor, jnp.broadcast_to(identity, system.shape), lower=True
    )
    root_part = math.sqrt(members - 1.0) * jnp.swapaxes(inverse, -1, -2)
    center = identity - 1.0 / members
    inner = mean_weight + inflation[:, None, None] * root_part
    return 1.0 / members + jnp.matmul(center, inner, precision=exact_mode)


def pick_cells(ensemble, block_ids, offsets):
    windows, members, cells_here = ensemble.shape
    blocks_count = cells_here // BLOCK
    requested = block_ids.shape[1]
    slots = offsets.shape[2]
    group = 64
    groups = requested // group
    grid = ensemble.reshape(windows, members, blocks_count, BLOCK)
    block_groups = block_ids.reshape(windows, groups, group)
    offset_groups = offsets.reshape(windows, groups, group, slots)
    block_range = jnp.arange(blocks_count, dtype=jnp.int32)
    cell_range = jnp.arange(BLOCK, dtype=jnp.int32)

    def one_window(packed):
        members_grid, window_blocks, window_offsets = packed

        def one_group(inner):
            group_blocks, group_offsets = inner
            block_hot = (group_blocks[:, None] == block_range[None, :]).astype(jnp.bfloat16)
            chosen = jnp.einsum(
                "qb,mbc->qmc", block_hot, members_grid, preferred_element_type=jnp.float32
            ).astype(jnp.bfloat16)
            slot_hot = (group_offsets[:, :, None] == cell_range[None, None, :]).astype(jnp.bfloat16)
            return jnp.einsum(
                "qmc,qsc->mqs", chosen, slot_hot, preferred_element_type=jnp.float32
            ).astype(jnp.bfloat16)

        parts = lax.map(one_group, (window_blocks, window_offsets))
        return jnp.moveaxis(parts, 0, 1).reshape(members, requested, slots)

    return lax.map(one_window, (grid, block_groups, offset_groups))


def partial_gram(observed_ens, values, weights):
    windows, members = (observed_ens.shape[0], observed_ens.shape[1])
    picked = observed_ens.reshape(windows, members, -1).astype(jnp.float32)
    flat_values = values.reshape(windows, -1)
    flat_weights = weights.reshape(windows, -1)
    average = jnp.mean(picked, axis=1)
    scaled = flat_weights[:, None, :] * (picked - average[:, None, :])
    innovation = flat_weights * (flat_values - average)
    gram_part = jnp.einsum("wmn,wkn->wmk", scaled, scaled, precision=exact_mode)
    projection = jnp.einsum("wmn,wn->wm", scaled, innovation, precision=exact_mode)
    return (gram_part, projection)


def combine(earlier, later):
    return jnp.matmul(later, earlier, precision=exact_mode)


def body(ensemble, obs_owner, obs_local, obs_offset, obs_count, obs_value, obs_var, inflation):
    windows, members, cells_here = ensemble.shape
    blocks_here = obs_local.shape[1]
    slots = obs_offset.shape[2]
    shards = lax.axis_size("space")
    capacity = 2 * blocks_here // shards
    owner_id = obs_owner[:, :, 0]
    one_hot = (owner_id[:, :, None] == jnp.arange(shards, dtype=jnp.int32)[None, None, :]).astype(
        jnp.float32
    )
    row_ids = jnp.arange(blocks_here, dtype=jnp.int32)
    lower_tri = (row_ids[None, :] < row_ids[:, None]).astype(jnp.float32)
    earlier_count = jnp.einsum("ij,wjs->wis", lower_tri, one_hot, precision=exact_mode)
    rank_in = jnp.sum(earlier_count * one_hot, axis=2).astype(jnp.int32)
    slot_of = owner_id * capacity + rank_in
    slot_range = jnp.arange(shards * capacity, dtype=jnp.int32)
    placer = (slot_of[:, :, None] == slot_range[None, None, :]).astype(jnp.float32)

    def place(source):
        tail_shape = source.shape[2:]
        flat = source.astype(jnp.float32).reshape(windows, blocks_here, -1)
        placed = jnp.einsum("wjq,wjt->wqt", placer, flat, precision=exact_mode)
        return placed.reshape((windows, shards, capacity) + tail_shape)

    live_slot = jnp.arange(slots, dtype=jnp.int32)[None, None, :] < obs_count[:, :, None]
    weight = jnp.where(live_slot, 1.0 / jnp.sqrt(obs_var), jnp.float32(0.0))
    value_slots = place(obs_value)
    weight_slots = place(weight)
    local_slots = place(obs_local).astype(jnp.int32)
    offset_slots = place(obs_offset).astype(jnp.int32)
    local_in, offset_in = (
        lax.all_to_all(local_slots, "space", split_axis=1, concat_axis=1, tiled=True),
        lax.all_to_all(offset_slots, "space", split_axis=1, concat_axis=1, tiled=True),
    )
    block_ids = local_in.reshape(windows, shards * capacity)
    offsets = offset_in.reshape(windows, shards * capacity, slots)
    picked = pick_cells(ensemble, block_ids, offsets).reshape(
        windows, members, shards, capacity * slots
    )
    observed_ens = lax.all_to_all(picked, "space", split_axis=2, concat_axis=2, tiled=True)
    gram_part, projection = partial_gram(observed_ens, value_slots, weight_slots)
    gram_sum, proj_sum = lax.psum((gram_part, projection), "space")
    transform = build_transform(gram_sum, proj_sum, inflation)
    identity = jnp.eye(members, dtype=jnp.float32)
    local_product = transform[0]
    turn = 1
    local_product = jnp.matmul(local_product, transform[turn], precision=exact_mode)
    suffix = carried_in(local_product, "tm", combine, identity)
    tail = suffix
    suffixes = []
    for turn in range(windows - 1, -1, -1):
        tail = jnp.matmul(transform[turn], tail, precision=exact_mode)
        suffixes.insert(0, tail)
    totals = jnp.stack(suffixes)
    return jnp.einsum("wmk,wmc->wkc", totals, ensemble.astype(jnp.float32), precision=exact_mode)


def solution(mesh):
    in_specs = (
        P("tm", None, "space"),
        P("tm", "space", None),
        P("tm", "space"),
        P("tm", "space", None),
        P("tm", "space"),
        P("tm", "space", None),
        P("tm", "space", None),
        P("tm"),
    )
    out_specs = P("tm", None, "space")
    return jax.shard_map(body, mesh=mesh, in_specs=in_specs, out_specs=out_specs, check_vma=False)
```

profile of v0, /device:TPU:8, one launch (start us, length us, event | category | flops | bytes accessed | tf_op | source)
XLA Modules:
  0.0 339.6 jit_solution(6430964338076641847)
XLA Ops:
  0.0 0.9 fusion.42
  0.9 0.7 multiply_add_fusion
  1.6 0.7 convert_element_type.66
  2.7 0.6 copy.71
  3.3 11.3 %all-to-all-start = ((s32[2,32,8]{2,0,1:T(2,128)}), s32[2,32,8]{2,0,1:T(2,128)S(1)}, u32[]{:S(2)}, u32[]{:S(2)}) async-start(s32[2,32,8]{2,0,1:T(2,128)} %copy.71), calls=%async_computation | async-start | bytes 65536 | tf_op jit(solution)/shard_map/all_to_all | solution.py:124
  14.6 1.0 convolution_convert_fusion.1
  15.8 0.8 reshape.93
  16.6 7.9 %all-to-all-done = s32[2,32,8]{2,0,1:T(2,128)S(1)} async-done(((s32[2,32,8]{2,0,1:T(2,128)}), s32[2,32,8]{2,0,1:T(2,128)S(1)}, u32[]{:S(2)}, u32[]{:S(2)}) %all-to-all-start) | async-done | bytes 2080 | tf_op jit(solution)/shard_map/all_to_all | solution.py:124
  24.6 3.8 %all-to-all-start.1 = ((s32[32,1,512]{2,1,0:T(1,128)}), s32[32,1,512]{2,1,0:T(1,128)S(1)}, u32[]{:S(2)}, u32[]{:S(2)}) async-start(s32[32,1,512]{2,1,0:T(1,128)} %reshape.93), calls=%async_computation.1 | async-start | bytes 131072 | tf_op jit(solution)/shard_map/all_to_all | solution.py:125
  28.4 5.3 %copy.98 = bf16[16,8,64,256]{3,2,1,0:T(8,128)(2,1)} copy(bf16[16,8,64,256]{3,1,2,0:T(8,128)(2,1)} %bitcast.140) | data formatting | bytes 8388608
  33.8 4.6 %all-to-all-done.1 = s32[32,1,512]{2,1,0:T(1,128)S(1)} async-done(((s32[32,1,512]{2,1,0:T(1,128)}), s32[32,1,512]{2,1,0:T(1,128)S(1)}, u32[]{:S(2)}, u32[]{:S(2)}) %all-to-all-start.1) | async-done | bytes 65568 | tf_op jit(solution)/shard_map/all_to_all | solution.py:125
  38.9 0.8 reduce.7
  39.9 44.3 %while.36 = (s32[]{:T(128)}, bf16[2,64,256,32]{1,3,2,0:T(8,128)(2,1)}, s32[2,4,64]{2,1,0:T(4,128)S(1)}, s32[2,4,64,32]{3,2,1,0:T(8,128)S(1)}, bf16[2,64,64,256]{...) while((s32[]{:T(128)}, bf16[2,64,256,32]{1,3,2,0:T(8,128)(2,1)}, ...), condition=%wide.region_4.5_spmd.clone, body=%wide.region_1.4_spmd.clone.sunk | while | flops 203034624 | bytes 15301126 | solution.py:73
  39.9 1.7 dynamic-slice_bitcast_fusion.10
  41.7 17.1 %while.37 = (s32[]{:T(128)}, bf16[4,64,64,32]{1,3,2,0:T(8,128)(2,1)}, s32[4,64,32]{2,1,0:T(8,128)S(1)}, s32[256]{0:T(256)S(1)}, s32[4,64]{1,0:T(4,128)S(1)}, /*i...) while((s32[]{:T(128)}, bf16[4,64,64,32]{1,3,2,0:T(8,128)(2,1)}, s32[4,64,32]{2,1,0:T(8,128)S(1)}, ...), condition=%wide.region_3.3_spmd, body=%wide.region_2.2_spmd.sunk | while | flops 203034624 | bytes 6842973 | solution.py:70
  41.7 0.8 convolution_convert_fusion.3
  42.5 3.5 %fusion.111 = bf16[4,64,64,32]{1,3,2,0:T(8,128)(2,1)} fusion(bf16[4,64,64,32]{1,3,2,0:T(8,128)(2,1)} %get-tuple-element.311, s32[]{:T(128)} %get-tuple-element.310, bf16[64,64,256]{2,0,1:T(8,128)(2,1)S(1)} %convolution_convert_fusion.3, s32[256]{0:T(256)S(1)} %get-tuple-element.321, s32[64,32]{1,0:T(8,128)S(1)} %dynamic-slice_bitcast_fusion.11), kind=kOutput, calls=%fused_computation.8.clone.1 | convolution fusion | flops 67764224 | bytes 2631168 | tf_op jit(solution)/shard_map/while/body/eval_jaxpr/while/body/eval_jaxpr/qmc,qsc->mqs/dot_general | solution.py:66
  46.0 0.8 convolution_convert_fusion.3
  46.7 3.5 %fusion.111 = bf16[4,64,64,32]{1,3,2,0:T(8,128)(2,1)} fusion(bf16[4,64,64,32]{1,3,2,0:T(8,128)(2,1)} %get-tuple-element.311, s32[]{:T(128)} %get-tuple-element.310, bf16[64,64,256]{2,0,1:T(8,128)(2,1)S(1)} %convolution_convert_fusion.3, s32[256]{0:T(256)S(1)} %get-tuple-element.321, s32[64,32]{1,0:T(8,128)S(1)} %dynamic-slice_bitcast_fusion.11), kind=kOutput, calls=%fused_computation.8.clone.1 | convolution fusion | flops 67764224 | bytes 2631168 | tf_op jit(solution)/shard_map/while/body/eval_jaxpr/while/body/eval_jaxpr/qmc,qsc->mqs/dot_general | solution.py:66
  50.2 0.7 convolution_convert_fusion.3
  51.0 3.5 %fusion.111 = bf16[4,64,64,32]{1,3,2,0:T(8,128)(2,1)} fusion(bf16[4,64,64,32]{1,3,2,0:T(8,128)(2,1)} %get-tuple-element.311, s32[]{:T(128)} %get-tuple-element.310, bf16[64,64,256]{2,0,1:T(8,128)(2,1)S(1)} %convolution_convert_fusion.3, s32[256]{0:T(256)S(1)} %get-tuple-element.321, s32[64,32]{1,0:T(8,128)S(1)} %dynamic-slice_bitcast_fusion.11), kind=kOutput, calls=%fused_computation.8.clone.1 | convolution fusion | flops 67764224 | bytes 2631168 | tf_op jit(solution)/shard_map/while/body/eval_jaxpr/while/body/eval_jaxpr/qmc,qsc->mqs/dot_general | solution.py:66
  54.5 0.8 convolution_convert_fusion.3
  55.3 3.5 %fusion.111 = bf16[4,64,64,32]{1,3,2,0:T(8,128)(2,1)} fusion(bf16[4,64,64,32]{1,3,2,0:T(8,128)(2,1)} %get-tuple-element.311, s32[]{:T(128)} %get-tuple-element.310, bf16[64,64,256]{2,0,1:T(8,128)(2,1)S(1)} %convolution_convert_fusion.3, s32[256]{0:T(256)S(1)} %get-tuple-element.321, s32[64,32]{1,0:T(8,128)S(1)} %dynamic-slice_bitcast_fusion.11), kind=kOutput, calls=%fused_computation.8.clone.1 | convolution fusion | flops 67764224 | bytes 2631168 | tf_op jit(solution)/shard_map/while/body/eval_jaxpr/while/body/eval_jaxpr/qmc,qsc->mqs/dot_general | solution.py:66
  58.7 3.3 bitcast_dynamic-update-slice_fusion.2
  62.0 1.7 dynamic-slice_bitcast_fusion.10
  63.8 17.1 %while.37 = (s32[]{:T(128)}, bf16[4,64,64,32]{1,3,2,0:T(8,128)(2,1)}, s32[4,64,32]{2,1,0:T(8,128)S(1)}, s32[256]{0:T(256)S(1)}, s32[4,64]{1,0:T(4,128)S(1)}, /*i...) while((s32[]{:T(128)}, bf16[4,64,64,32]{1,3,2,0:T(8,128)(2,1)}, s32[4,64,32]{2,1,0:T(8,128)S(1)}, ...), condition=%wide.region_3.3_spmd, body=%wide.region_2.2_spmd.sunk | while | flops 203034624 | bytes 6842973 | solution.py:70
  63.8 0.7 convolution_convert_fusion.3
  64.6 3.5 %fusion.111 = bf16[4,64,64,32]{1,3,2,0:T(8,128)(2,1)} fusion(bf16[4,64,64,32]{1,3,2,0:T(8,128)(2,1)} %get-tuple-element.311, s32[]{:T(128)} %get-tuple-element.310, bf16[64,64,256]{2,0,1:T(8,128)(2,1)S(1)} %convolution_convert_fusion.3, s32[256]{0:T(256)S(1)} %get-tuple-element.321, s32[64,32]{1,0:T(8,128)S(1)} %dynamic-slice_bitcast_fusion.11), kind=kOutput, calls=%fused_computation.8.clone.1 | convolution fusion | flops 67764224 | bytes 2631168 | tf_op jit(solution)/shard_map/while/body/eval_jaxpr/while/body/eval_jaxpr/qmc,qsc->mqs/dot_general | solution.py:66
  68.1 0.7 convolution_convert_fusion.3
  68.9 3.5 %fusion.111 = bf16[4,64,64,32]{1,3,2,0:T(8,128)(2,1)} fusion(bf16[4,64,64,32]{1,3,2,0:T(8,128)(2,1)} %get-tuple-element.311, s32[]{:T(128)} %get-tuple-element.310, bf16[64,64,256]{2,0,1:T(8,128)(2,1)S(1)} %convolution_convert_fusion.3, s32[256]{0:T(256)S(1)} %get-tuple-element.321, s32[64,32]{1,0:T(8,128)S(1)} %dynamic-slice_bitcast_fusion.11), kind=kOutput, calls=%fused_computation.8.clone.1 | convolution fusion | flops 67764224 | bytes 2631168 | tf_op jit(solution)/shard_map/while/body/eval_jaxpr/while/body/eval_jaxpr/qmc,qsc->mqs/dot_general | solution.py:66
  72.4 0.8 convolution_convert_fusion.3
  73.1 3.5 %fusion.111 = bf16[4,64,64,32]{1,3,2,0:T(8,128)(2,1)} fusion(bf16[4,64,64,32]{1,3,2,0:T(8,128)(2,1)} %get-tuple-element.311, s32[]{:T(128)} %get-tuple-element.310, bf16[64,64,256]{2,0,1:T(8,128)(2,1)S(1)} %convolution_convert_fusion.3, s32[256]{0:T(256)S(1)} %get-tuple-element.321, s32[64,32]{1,0:T(8,128)S(1)} %dynamic-slice_bitcast_fusion.11), kind=kOutput, calls=%fused_computation.8.clone.1 | convolution fusion | flops 67764224 | bytes 2631168 | tf_op jit(solution)/shard_map/while/body/eval_jaxpr/while/body/eval_jaxpr/qmc,qsc->mqs/dot_general | solution.py:66
  76.6 0.7 convolution_convert_fusion.3
  77.4 3.5 %fusion.111 = bf16[4,64,64,32]{1,3,2,0:T(8,128)(2,1)} fusion(bf16[4,64,64,32]{1,3,2,0:T(8,128)(2,1)} %get-tuple-element.311, s32[]{:T(128)} %get-tuple-element.310, bf16[64,64,256]{2,0,1:T(8,128)(2,1)S(1)} %convolution_convert_fusion.3, s32[256]{0:T(256)S(1)} %get-tuple-element.321, s32[64,32]{1,0:T(8,128)S(1)} %dynamic-slice_bitcast_fusion.11), kind=kOutput, calls=%fused_computation.8.clone.1 | convolution fusion | flops 67764224 | bytes 2631168 | tf_op jit(solution)/shard_map/while/body/eval_jaxpr/while/body/eval_jaxpr/qmc,qsc->mqs/dot_general | solution.py:66
  80.9 3.3 bitcast_dynamic-update-slice_fusion.2
  84.2 4.8 %copy.76 = bf16[2,64,32,256]{3,1,0,2:T(8,128)(2,1)} copy(bf16[2,64,32,256]{1,3,2,0:T(8,128)(2,1)} %bitcast.141) | data formatting | bytes 4194304 | tf_op jit(solution)/shard_map/reshape | solution.py:129
  88.9 5.5 %all-to-all-start.2 = ((bf16[2,64,32,256]{3,1,0,2:T(8,128)(2,1)}), bf16[2,64,32,256]{3,1,0,2:T(8,128)(2,1)S(1)}, u32[]{:S(2)}, u32[]{:S(2)}) async-start(bf16[2,64,32,256]{3,1,0,2:T(8,128)(2,1)} %copy.76), calls=%async_computation.2 | async-start | bytes 4194304 | tf_op jit(solution)/shard_map/all_to_all | solution.py:132
  95.9 47.2 %all-to-all-done.2 = bf16[2,64,32,256]{3,1,0,2:T(8,128)(2,1)S(1)} async-done(((bf16[2,64,32,256]{3,1,0,2:T(8,128)(2,1)}), bf16[2,64,32,256]{3,1,0,2:T(8,128)(2,1)S(1)}, u32[]{:S(2)}, u32[]{:S(2)}) %all-to-all-start.2) | async-done | bytes 2097184 | tf_op jit(solution)/shard_map/all_to_all | solution.py:132
  143.0 0.6 convert_reduce_fusion
  143.7 0.5 convert_bitcast_fusion
  144.7 4.1 %fusion.34 = f32[2,64,64]{1,2,0:T(8,128)S(1)} fusion(f32[2,64,8192]{2,1,0:T(8,128)S(1)} %bitcast.138, f32[2,8192]{1,0:T(2,128)S(1)} %bitcast.144, f32[2,8192]{1,0:T(2,128)S(1)} %mul.48), kind=kOutput, calls=%fused_computation.30 | convolution fusion | flops 807403520 | bytes 4358144 | tf_op jit(solution)/shard_map/wmn,wkn->wmk/dot_general | solution.py:84
  148.9 3.9 %fusion.33 = f32[2,1,64]{2,1,0:T(1,128)S(1)} fusion(f32[2,64,8192]{2,1,0:T(8,128)S(1)} %bitcast.139, f32[2,8192]{1,0:T(2,128)S(1)} %bitcast.145, f32[2,8192]{1,0:T(2,128)S(1)} %mul.48, f32[2,8192,1]{1,0,2:T(2,128)S(1)} %multiply_bitcast_fusion), kind=kOutput, calls=%fused_computation.29 | convolution fusion | flops 14680064 | bytes 4391424 | tf_op jit(solution)/shard_map/wmn,wn->wm/dot_general | solution.py:85
  152.8 140.4 %all-reduce = (f32[2,64,64]{1,2,0:T(8,128)S(1)}, f32[2,64]{1,0:T(2,128)S(1)}) all-reduce(f32[2,64,64]{1,2,0:T(8,128)S(1)} %fusion.34, f32[2,64]{1,0:T(2,128)S(1)} %bitcast.153), channel_id=1, replica_groups=mesh['tm'=8,'space'=32] {'space'}, use_global_device_ids=true, to_apply=%region_6.7 | all-reduce | flops 8320 | bytes 66560 | tf_op jit(solution)/shard_map/psum | solution.py:134
  293.3 11.7 %custom-call.14 = f32[2,64,64]{2,1,0:T(8,128)S(1)} custom-call(f32[2,64,64]{2,1,0:T(8,128)S(1)} %fusion.61), custom_call_target="Cholesky" | custom-call | tf_op jit(solution)/shard_map/jit(cholesky)/cholesky | solution.py:32
  305.3 9.8 %custom-call.15 = f32[2,1,64,64]{2,3,1,0:T(8,128)S(1)} custom-call(f32[2,1,64,64]{3,2,1,0:T(8,128)S(1)} %select_bitcast_fusion), custom_call_target="InvertDiagBlocksLowerTriangular" | custom-call | tf_op jit(solution)/shard_map/jit(_cho_solve)/vmap()/triangular_solve | solution.py:33
  316.1 13.1 %all-gather = f32[512,64]{1,0:T(8,128)S(1)} all-gather(f32[64,64]{1,0:T(8,128)S(1)} %fusion.71), channel_id=2, replica_groups=mesh['tm'=8,'space'=32] {'tm'}, dimensions={0}, use_global_device_ids=true | all-gather | bytes 147456 | tf_op jit(solution)/shard_map/all_gather | solution.py:18
  329.2 1.0 while.34
  330.5 9.1 %fusion.53 = f32[2,64,16384]{2,1,0:T(8,128)} fusion(bf16[2,64,16384]{2,1,0:T(8,128)(2,1)} %param.14, f32[1,64,64]{2,1,0:T(8,128)S(1)} %bitcast.148, f32[1,64,64]{2,1,0:T(8,128)S(1)} %convolution_bitcast_fusion), kind=kOutput, calls=%fused_computation.54 | convolution fusion | flops 1610620928 | bytes 12615680 | tf_op jit(solution)/shard_map/wmk,wmc->wkc/dot_general | solution.py:147
  (83 shorter events, 5.7 us)
Async XLA Ops:
  0.0 95.1 %copy-start = (f32[2,128,32]{1,2,0:T(8,128)S(1)}, f32[2,128,32]{1,2,0:T(8,128)}, u32[]{:S(2)}) copy-start(f32[2,128,32]{1,2,0:T(8,128)} %param.19) | copy-start | bytes 98308
  3.3 21.2 %all-to-all-start = ((s32[2,32,8]{2,0,1:T(2,128)}), s32[2,32,8]{2,0,1:T(2,128)S(1)}, u32[]{:S(2)}, u32[]{:S(2)}) async-start(s32[2,32,8]{2,0,1:T(2,128)} %copy.71), calls=%async_computation | async-start | bytes 65536 | tf_op jit(solution)/shard_map/all_to_all | solution.py:124
  24.6 13.9 %all-to-all-start.1 = ((s32[32,1,512]{2,1,0:T(1,128)}), s32[32,1,512]{2,1,0:T(1,128)S(1)}, u32[]{:S(2)}, u32[]{:S(2)}) async-start(s32[32,1,512]{2,1,0:T(1,128)} %reshape.93), calls=%async_computation.1 | async-start | bytes 131072 | tf_op jit(solution)/shard_map/all_to_all | solution.py:125
  84.1 10.3 %copy-start.1 = (f32[2,128,32]{1,2,0:T(8,128)S(1)}, f32[2,128,32]{1,2,0:T(8,128)}, u32[]{:S(2)}) copy-start(f32[2,128,32]{1,2,0:T(8,128)} %param.20) | copy-start | bytes 98308
  84.1 10.3 %copy-start.2 = (s32[2,128]{1,0:T(2,128)S(1)}, s32[2,128]{1,0:T(2,128)}, u32[]{:S(2)}) copy-start(s32[2,128]{1,0:T(2,128)} %param.18) | copy-start | bytes 3076
  88.9 6.9 %copy-start.3 = (f32[2]{0:T(128)S(1)}, f32[2]{0:T(128)}, u32[]{:S(2)}) copy-start(f32[2]{0:T(128)} %param.21) | copy-start | bytes 28
  88.9 54.1 %all-to-all-start.2 = ((bf16[2,64,32,256]{3,1,0,2:T(8,128)(2,1)}), bf16[2,64,32,256]{3,1,0,2:T(8,128)(2,1)S(1)}, u32[]{:S(2)}, u32[]{:S(2)}) async-start(bf16[2,64,32,256]{3,1,0,2:T(8,128)(2,1)} %copy.76), calls=%async_computation.2 | async-start | bytes 4194304 | tf_op jit(solution)/shard_map/all_to_all | solution.py:132
where the time goes:
time: 342 us; the launch traced here: 340 us
  blocking collectives  153 us (45%)
  waiting for transfers between devices  59.7 us (17%)
  matrix products  56 us (16%)
  other arithmetic  25.2 us (7%)
  local copies, waits for them, and re-layouts  23.8 us (7%)
  starting transfers between devices  20.7 us (6%)
    psum x1, blocking collectives, body(): gram_sum, proj_sum = lax.psum((gram_part, projection), 'space')  140 us
    all_to_all x1, waiting for transfers between devices, body(): lax.all_to_all(picked, 'space', split_axis=2, concat_axis=2, tiled=True)  47.2 us
    dot_general x8, matrix products, one_group(): jnp.einsum('qmc,qsc->mqs', chosen, slot_hot, preferred_element_type=jnp.f...  27.9 us
    all_gather x1, blocking collectives, carried_in(): gathered = lax.all_gather(part, axis)  13.1 us
    another operation x3, other arithmetic, build_transform(): factor = jnp.linalg.cholesky(system)  11.9 us
    all_to_all x1, starting transfers between devices, body(): lax.all_to_all(local_slots, 'space', split_axis=1, concat_axis=1, tiled=T...  11.3 us
    another operation x3, other arithmetic, build_transform(): jax.scipy.linalg.cho_solve((factor, True), projection[..., None])  9.92 us
    dot_general x1, matrix products, body(): jnp.einsum('wmk,wmc->wkc', totals, ensemble.astype(jnp.float32), precisio...  9.06 us
  transfers between devices with their start and end apart: 3, of which 3 were waited for; matrix products, arithmetic and copies ran while one was open for 3% of the time, Pallas kernels for 0%

commit v1 on v0

v1 whole, which is shorter than its diff:
```python
import math

import jax
import jax.numpy as jnp
from jax import lax
from jax.experimental import pallas as pl
from jax.experimental.pallas import tpu as pltpu
from jax.sharding import PartitionSpec as P

MEMB = 64
BLOCK = 256
SLOTS = 32
CAP = 8
SHARDS = 32
NBLK = 64
CELLS = NBLK * BLOCK
ROWS = 40
STEP = 8
DEPTH = 4096
WIDTH = 4096

f32 = jnp.float32
bf16 = jnp.bfloat16
exact_mode = lax.Precision.HIGHEST
NT = (((1,), (1,)), ((), ()))


def iota(shape, dim):
    return lax.broadcasted_iota(jnp.int32, shape, dim)


def split(x):
    hi = x.astype(bf16)
    return hi, (x - hi.astype(f32)).astype(bf16)


def route_kernel(owner_ref, local_ref, offset_ref, count_ref, value_ref, var_ref, out_ref):
    for w in range(2):
        owner = owner_ref[w : w + 1, :]
        across = jnp.broadcast_to(owner, (128, 128))
        same = jnp.where((across == across.T) & (iota((128, 128), 0) < iota((128, 128), 1)), 1.0, 0.0)
        rank = jnp.sum(same, axis=0, keepdims=True).astype(jnp.int32)
        target = owner * CAP + rank
        placer = jnp.where(iota((SHARDS * CAP, 128), 0) == target, 1.0, 0.0).astype(bf16)
        live = iota((SLOTS, 128), 0) < count_ref[w : w + 1, :]
        precision = jnp.where(live, 1.0 / var_ref[w], 0.0)
        rows = jnp.concatenate(
            [
                precision,
                precision * value_ref[w],
                offset_ref[w].astype(f32),
                jnp.broadcast_to(local_ref[w : w + 1, :], (SLOTS, 128)).astype(f32),
            ],
            axis=0,
        )
        high = rows.astype(bf16)
        rest = rows - high.astype(f32)
        middle = rest.astype(bf16)
        low = (rest - middle.astype(f32)).astype(bf16)
        placed = sum(
            lax.dot_general(placer, part, NT, preferred_element_type=f32) for part in (low, middle, high)
        )
        out_ref[:, w * CAP : (w + 1) * CAP, :] = placed.reshape(SHARDS, CAP, 128)


def center_kernel(ens_hbm, mean_ref, ens, sems):
    copies = [
        pltpu.make_async_copy(
            ens_hbm.at[i // 4, :, pl.ds(i % 4 * 4096, 4096)], ens.at[i // 4, :, pl.ds(i % 4 * 4096, 4096)], sems.at[i]
        )
        for i in range(8)
    ]
    for copy in copies:
        copy.start()
    for i in range(8):
        copies[i].wait()

        def some(step, carry):
            block = i % 4 * 16 + step * 8
            for k in range(8):
                where = pl.ds(pl.multiple_of((block + k) * BLOCK, BLOCK), BLOCK)
                members = ens[i // 4, :, where].astype(f32)
                mean_ref[i // 4, pl.ds(block + k, 1), :] = jnp.sum(members, axis=0, keepdims=True) * (1.0 / MEMB)
            return carry

        lax.fori_loop(0, 2, some, 0)


def gram_kernel(recv_ref, mean_ref, ens_hbm, out_ref, ens, sems, table, dense, scale, ratio, scaled):
    copies = [pltpu.make_async_copy(ens_hbm.at[w], ens.at[w], sems.at[w]) for w in range(2)]
    for copy in copies:
        copy.start()
    for w in range(2):
        table[w] = recv_ref[:, w * CAP : (w + 1) * CAP, :].reshape(SHARDS * CAP, 128).T
    for w in range(2):

        def scatter(tile, carry):
            base = pl.multiple_of(tile * 32, 32)
            cells = (iota((32, 256), 0) + base).astype(f32)
            acc_u = jnp.zeros((32, 256), f32)
            acc_t = jnp.zeros((32, 256), f32)
            for s in range(SLOTS):
                hit = table[w, 64 + s : 65 + s, :] == cells
                acc_u += jnp.where(hit, table[w, s : s + 1, :], 0.0)
                acc_t += jnp.where(hit, table[w, 32 + s : 33 + s, :], 0.0)
            dense[w, pl.ds(base, 32), :] = acc_u
            dense[w, pl.ds(base + 256, 32), :] = acc_t
            return carry

        lax.fori_loop(0, 8, scatter, 0)
    for w in range(2):
        held = jnp.where(iota((NBLK, 256), 0).astype(f32) == table[w, 96:97, :], 1.0, 0.0).astype(bf16)
        placed = sum(lax.dot_general(held, part, NT, preferred_element_type=f32) for part in split(dense[w])[::-1])
        total = placed[:, :256]
        root = jnp.sqrt(total)
        scale[w] = root
        ratio[w] = jnp.where(total > 0.0, (placed[:, 256:] - total * mean_ref[w]) / root, 0.0)
    row16 = iota((16, BLOCK), 0)
    fulls = []
    for w in range(2):
        copies[w].wait()

        def fill(step, carry):
            for k in range(8):
                b = step * 8 + k
                where = pl.ds(pl.multiple_of(b * BLOCK, BLOCK), BLOCK)
                deviations = ens[w, :, where].astype(f32) - mean_ref[w, pl.ds(b, 1), :]
                high, low = split(deviations * scale[w, pl.ds(b, 1), :])
                scaled[w, 16 : 16 + MEMB, where] = high
                scaled[w, 16 + MEMB :, where] = low
                extra = ratio[w, pl.ds(b, 1), :]
                top = extra.astype(bf16).astype(f32)
                scaled[w, 0:16, where] = jnp.where(
                    row16 == 0, top, jnp.where(row16 == 1, extra - top, 0.0)
                ).astype(bf16)
            return carry

        lax.fori_loop(0, NBLK // 8, fill, 0)

        def product(step, acc):
            where = pl.ds(pl.multiple_of(step * DEPTH, DEPTH), DEPTH)
            return acc + lax.dot_general(
                scaled[w, 16:, where], scaled[w, : MEMB + 16, where], NT, preferred_element_type=f32
            )

        fulls.append(lax.fori_loop(0, CELLS // DEPTH, product, jnp.zeros((2 * MEMB, MEMB + 16), f32)))
    packs = []
    for full in fulls:
        cross = full[MEMB:, 16:]
        gram = full[:MEMB, 16:] + (cross + cross.T)
        both = full[:MEMB] + full[MEMB:]
        packs.append((gram, both[:, :1] + both[:, 1:2]))
    row, col = iota((MEMB, MEMB), 0), iota((MEMB, MEMB), 1)

    def as_row(values):
        return jnp.sum(jnp.where(row == col, values, 0.0), axis=0, keepdims=True)

    mixed = jnp.where(row <= col, packs[0][0], packs[1][0])
    body = jnp.concatenate([mixed[:32], mixed[32:]], axis=1)
    first = jnp.concatenate([as_row(packs[1][0]), as_row(packs[0][1])], axis=1)
    second = jnp.concatenate([as_row(packs[1][1]), jnp.zeros((1, MEMB), f32)], axis=1)
    packed = jnp.concatenate([body, first, second, jnp.zeros((ROWS - 34, 128), f32)], axis=0)
    out_ref[...] = jnp.broadcast_to(packed[None], (SHARDS, ROWS, 128))


def eliminate(systems):
    row, lane = iota((MEMB, 2 * MEMB), 0), iota((MEMB, 2 * MEMB), 1)
    eye = jnp.where(row + MEMB == lane, 1.0, 0.0)
    count = len(systems)
    tiles = []
    for system in systems:
        wide = jnp.concatenate([system, jnp.zeros((MEMB, MEMB), f32)], axis=1) + eye
        tiles.append([wide[8 * i : 8 * i + 8] for i in range(MEMB // 8)])
    found = [[] for _ in systems]
    full = (8, 2 * MEMB)
    for j in range(0, MEMB, STEP):
        t, s = divmod(j, 8)
        for w in range(count):
            rows = [jnp.broadcast_to(tiles[w][t][s + k : s + k + 1, :], full) for k in range(STEP)]
            block = [
                [jnp.broadcast_to(rows[k][:, j + l : j + l + 1], full) if l >= k else None for l in range(STEP)]
                for k in range(STEP)
            ]
            inverses, lower = [], [[None] * STEP for _ in range(STEP)]
            for k in range(STEP):
                inv = 1.0 / block[k][k]
                inverses.append(inv)
                for l in range(k + 1, STEP):
                    lower[l][k] = block[k][l] * inv
                for l in range(k + 1, STEP):
                    for m in range(l, STEP):
                        block[l][m] = block[l][m] - lower[l][k] * block[k][m]
                    rows[l] = rows[l] - lower[l][k] * rows[k]
            for k in range(STEP):
                found[w].append(rows[k][:1, :] * lax.rsqrt(block[k][k][:1, :]))
            first = t if s + STEP < 8 else t + 1
            if first == MEMB // 8:
                continue
            solved = [None] * STEP
            for k in reversed(range(STEP)):
                value = rows[k] * inverses[k]
                for l in range(k + 1, STEP):
                    value = value - lower[l][k] * solved[l]
                solved[k] = value
            for i in range(first, MEMB // 8):
                tile = tiles[w][i]
                change = None
                for k in range(STEP):
                    part = jnp.broadcast_to(tile[:, j + k : j + k + 1], full) * solved[k]
                    change = part if change is None else change + part
                tiles[w][i] = tile - change
    return [jnp.concatenate(rows, axis=0)[:, MEMB:] for rows in found]


def transform_kernel(infl_ref, parts_ref, out_ref, product_ref):
    total = jnp.sum(parts_ref[...], axis=0)
    mixed = jnp.concatenate([total[:32, :MEMB], total[:32, MEMB:]], axis=0)
    other = mixed.T
    row, col = iota((MEMB, MEMB), 0), iota((MEMB, MEMB), 1)
    diag = jnp.where(row == col, total[32:33, :MEMB], 0.0)
    grams = [jnp.where(row <= col, mixed, other), jnp.where(row > col, mixed, jnp.where(row < col, other, diag))]
    projs = [total[32:33, MEMB:], total[33:34, :MEMB]]
    ridge = jnp.where(row == col, MEMB - 1.0, 0.0)
    result = []
    for w, inverse in enumerate(eliminate([gram + ridge for gram in grams])):
        half = jnp.sum(inverse * projs[w], axis=1, keepdims=True)
        weight = jnp.sum(inverse * half, axis=0, keepdims=True)
        inner = weight + (infl_ref[w] * math.sqrt(MEMB - 1.0)) * inverse
        result.append(1.0 / MEMB + inner - jnp.sum(inner, axis=1, keepdims=True) * (1.0 / MEMB))
    out_ref[0] = result[0]
    out_ref[1] = result[1]
    product_ref[...] = exact(result[1], result[0])


def exact(a, b):
    return jnp.dot(a, b, precision=exact_mode, preferred_element_type=f32)


def apply_kernel(suffix_ref, made_ref, ens_hbm, out_hbm, ens, out, in_sems, out_sems):
    pieces = 16384 // WIDTH

    def part(i):
        return (i // pieces, slice(None), pl.ds(i % pieces * WIDTH, WIDTH))

    reads = [pltpu.make_async_copy(ens_hbm.at[part(i)], ens.at[i], in_sems.at[i]) for i in range(2 * pieces)]
    for copy in reads:
        copy.start()
    last = exact(suffix_ref[...], made_ref[1])
    totals = [exact(last, made_ref[0]), last]
    writes = []
    for i in range(2 * pieces):
        reads[i].wait()
        both = jnp.concatenate(split(totals[i // pieces]), axis=1)
        cells = ens[i]
        out[i] = jnp.dot(both, jnp.concatenate([cells, cells], axis=0), preferred_element_type=f32)
        writes.append(pltpu.make_async_copy(out.at[i], out_hbm.at[part(i)], out_sems.at[i]))
        writes[i].start()
    for copy in writes:
        copy.wait()


def times(a, b):
    return jnp.matmul(a, b, precision=exact_mode)


def body(ensemble, obs_owner, obs_local, obs_offset, obs_count, obs_value, obs_var, inflation):
    vmem = pl.BlockSpec(memory_space=pltpu.VMEM)
    turned = lambda a: jnp.swapaxes(a, 1, 2)
    routed = pl.pallas_call(
        route_kernel,
        out_shape=pltpu.VMEM((SHARDS, 2 * CAP, 128), f32),
        in_specs=[vmem] * 6,
        out_specs=vmem,
        name="route",
    )(obs_owner[:, :, 0], obs_local, turned(obs_offset), obs_count, turned(obs_value), turned(obs_var))
    recv = lax.all_to_all(routed, "space", split_axis=0, concat_axis=0, tiled=True)
    ensemble = pltpu.with_memory_space_constraint(ensemble, pltpu.HBM)
    means = pl.pallas_call(
        center_kernel,
        out_shape=pltpu.VMEM((2, NBLK, BLOCK), f32),
        in_specs=[pl.BlockSpec(memory_space=pl.ANY)],
        out_specs=vmem,
        scratch_shapes=[pltpu.VMEM((2, MEMB, CELLS), bf16), pltpu.SemaphoreType.DMA((8,))],
        compiler_params=pltpu.CompilerParams(vmem_limit_bytes=20 * 2**20),
        name="center",
    )(ensemble)
    partial = pl.pallas_call(
        gram_kernel,
        out_shape=pltpu.VMEM((SHARDS, ROWS, 128), f32),
        in_specs=[vmem, vmem, pl.BlockSpec(memory_space=pl.ANY)],
        out_specs=vmem,
        scratch_shapes=[
            pltpu.VMEM((2, MEMB, CELLS), bf16),
            pltpu.SemaphoreType.DMA((2,)),
            pltpu.VMEM((2, 128, 256), f32),
            pltpu.VMEM((2, 512, 256), f32),
            pltpu.VMEM((2, NBLK, BLOCK), f32),
            pltpu.VMEM((2, NBLK, BLOCK), f32),
            pltpu.VMEM((2, 2 * MEMB + 16, CELLS), bf16),
        ],
        compiler_params=pltpu.CompilerParams(vmem_limit_bytes=30 * 2**20),
        name="gram",
    )(recv, means, ensemble)
    parts = lax.all_to_all(partial, "space", split_axis=0, concat_axis=0, tiled=True)
    made, product = pl.pallas_call(
        transform_kernel,
        out_shape=(pltpu.VMEM((2, MEMB, MEMB), f32), pltpu.VMEM((MEMB, MEMB), f32)),
        in_specs=[pl.BlockSpec(memory_space=pltpu.SMEM), vmem],
        out_specs=(vmem, vmem),
        compiler_params=pltpu.CompilerParams(vmem_limit_bytes=20 * 2**20),
        name="transform",
    )(inflation, parts)
    place = lax.axis_index("tm")
    eye = jnp.eye(MEMB, dtype=f32)
    suffix = eye
    for bit in (1, 2, 4):
        other = lax.ppermute(product, "tm", [(i, i ^ bit) for i in range(8)])
        first = (place & bit) == 0
        ahead = jnp.where(first, other, eye)
        suffix = ahead if bit == 1 else times(ahead, suffix)
        if bit < 4:
            product = times(jnp.where(first, other, product), jnp.where(first, product, other))
    return pl.pallas_call(
        apply_kernel,
        out_shape=jax.ShapeDtypeStruct((2, MEMB, CELLS), f32),
        in_specs=[vmem, vmem, pl.BlockSpec(memory_space=pl.ANY)],
        out_specs=pl.BlockSpec(memory_space=pl.ANY),
        scratch_shapes=[
            pltpu.VMEM((2 * CELLS // WIDTH, MEMB, WIDTH), bf16),
            pltpu.VMEM((2 * CELLS // WIDTH, MEMB, WIDTH), f32),
            pltpu.SemaphoreType.DMA((2 * CELLS // WIDTH,)),
            pltpu.SemaphoreType.DMA((2 * CELLS // WIDTH,)),
        ],
        compiler_params=pltpu.CompilerParams(vmem_limit_bytes=30 * 2**20),
        name="apply",
    )(suffix, made, ensemble)


def solution(mesh):
    in_specs = (
        P("tm", None, "space"),
        P("tm", "space", None),
        P("tm", "space"),
        P("tm", "space", None),
        P("tm", "space"),
        P("tm", "space", None),
        P("tm", "space", None),
        P("tm"),
    )
    out_specs = P("tm", None, "space")
    return jax.shard_map(body, mesh=mesh, in_specs=in_specs, out_specs=out_specs, check_vma=False)
```

time: 342 us -> 80.6 us (0.24)
  blocking collectives: 153 us -> 23.8 us
  matrix products: 56 us -> 0.65 us
  waiting for transfers between devices: 59.7 us -> 17.7 us
  other arithmetic: 25.2 us -> 0 us
  Pallas kernels: 0 us -> 23.8 us
  local copies, waits for them, and re-layouts: 23.8 us -> 0.01 us
  starting transfers between devices: 20.7 us -> 14.3 us
    psum x1 -> x0, blocking collectives: 140 us -> none  [body(): gram_sum, proj_sum = lax.psum((gram_part, projection), 'space')]
    dot_general x33 -> x4, matrix products: 55.4 us -> 0.65 us  [times(): return jnp.matmul(a, b, precision=exact_mode)]
    all_to_all x3 -> x1, waiting for transfers between devices: 59.7 us -> 10.1 us  [body(): lax.all_to_all(routed, 'space', split_axis=0, concat_axis=0, tiled=True)]
    all_to_all x0 -> x1, blocking collectives: none -> 23.8 us  [body(): lax.all_to_all(partial, 'space', split_axis=0, concat_axis=0, tiled=True)]
    pallas_call x0 -> x5, Pallas kernels: none -> 23.8 us  [the longest x1 10.6 us: body(): pl.pallas_call(gram_kernel, out_shape=pltpu.VMEM((SHARDS, ROWS, 128), f32...]
    another operation x8 -> x0, other arithmetic: 21.8 us -> none  [the longest x3 11.9 us: build_transform(): factor = jnp.linalg.cholesky(system)]
    all_gather x1 -> x0, blocking collectives: 13.1 us -> none  [carried_in(): gathered = lax.all_gather(part, axis)]
    all_to_all x3 -> x1, starting transfers between devices: 20.7 us -> 11.3 us  [body(): lax.all_to_all(routed, 'space', split_axis=0, concat_axis=0, tiled=True)]
  transfers between devices with their start and end apart: 3 -> 4, of which waited for: 3 -> 4; matrix products, arithmetic and copies ran while one was open for 3% -> 0% of each run, Pallas kernels for 0% -> 3%
where the time goes in v1:
time: 80.6 us; the launch traced here: 80.4 us
  Pallas kernels  23.8 us (30%)
  blocking collectives  23.8 us (30%)
  waiting for transfers between devices  17.7 us (22%)
  starting transfers between devices  14.3 us (18%)
    all_to_all x1, blocking collectives, body(): lax.all_to_all(partial, 'space', split_axis=0, concat_axis=0, tiled=True)  23.8 us
    all_to_all x1, starting transfers between devices, body(): lax.all_to_all(routed, 'space', split_axis=0, concat_axis=0, tiled=True)  11.3 us
    pallas_call x1, Pallas kernels, body(): pl.pallas_call(gram_kernel, out_shape=pltpu.VMEM((SHARDS, ROWS, 128), f32...  10.6 us
    all_to_all x1, waiting for transfers between devices, body(): lax.all_to_all(routed, 'space', split_axis=0, concat_axis=0, tiled=True)  10.1 us
    ppermute x3, waiting for transfers between devices, body(): other = lax.ppermute(product, 'tm', [(i, i ^ bit) for i in range(8)])  7.64 us
    pallas_call x1, Pallas kernels, body(): pl.pallas_call(apply_kernel, out_shape=jax.ShapeDtypeStruct((2, MEMB, CEL...  4.89 us
    pallas_call x1, Pallas kernels, body(): pl.pallas_call(transform_kernel, out_shape=(pltpu.VMEM((2, MEMB, MEMB), f...  4.01 us
    ppermute x3, starting transfers between devices, body(): other = lax.ppermute(product, 'tm', [(i, i ^ bit) for i in range(8)])  2.97 us
  transfers between devices with their start and end apart: 4, of which 4 were waited for; matrix products, arithmetic and copies ran while one was open for 0% of the time, Pallas kernels for 3%

profile of v1, /device:TPU:8, one launch (start us, length us, event | category | flops | bytes accessed | tf_op | source)
XLA Modules:
  0.0 80.4 jit_solution(2441077621395074785)
XLA Ops:
  0.0 0.0 copy-start
  0.0 1.9 %route.1 = f32[32,16,128]{2,1,0:T(8,128)} custom-call(s32[2,128]{1,0:T(2,128)} %bitcast.8, s32[2,128]{1,0:T(2,128)} %local_ref.1, s32[2,32,128]{2,1,0:T(8,128)} %bitcast.5, s32[2,128]{1,0:T(2,128)} %count_ref.1, f32[2,32,128]{2,1,0:T(8,128)} %bitcast.6, f32[2,32,128]{2,1,0:T(8,128)} %bitcast.7), custom_call_target="tpu_custom_call" | custom-call | tf_op jit(solution)/shard_map/route/pallas_call | solution.py:269
  1.9 11.3 %all-to-all-start = ((f32[32,16,128]{2,1,0:T(8,128)}), f32[32,16,128]{2,1,0:T(8,128)S(1)}, u32[]{:S(2)}, u32[]{:S(2)}) async-start(f32[32,16,128]{2,1,0:T(8,128)} %route.1), calls=%async_computation | async-start | bytes 524288 | tf_op jit(solution)/shard_map/all_to_all | solution.py:276
  13.2 2.3 %center.1.mean_ref = f32[2,64,256]{2,1,0:T(8,128)S(1)} custom-call(bf16[2,64,16384]{2,1,0:T(8,128)(2,1)} %ens_hbm.5), custom_call_target="tpu_custom_call" | custom-call | tf_op jit(solution)/shard_map/center/pallas_call | solution.py:278
  15.6 10.1 %all-to-all-done.recv_ref = f32[32,16,128]{2,1,0:T(8,128)S(1)} async-done(((f32[32,16,128]{2,1,0:T(8,128)}), f32[32,16,128]{2,1,0:T(8,128)S(1)}, u32[]{:S(2)}, u32[]{:S(2)}) %all-to-all-start) | async-done | bytes 262176 | tf_op jit(solution)/shard_map/all_to_all | solution.py:276
  25.7 10.6 %gram.1 = f32[32,40,128]{2,1,0:T(8,128)S(1)} custom-call(f32[32,16,128]{2,1,0:T(8,128)S(1)} %all-to-all-done.recv_ref, f32[2,64,256]{2,1,0:T(8,128)S(1)} %center.1.mean_ref, bf16[2,64,16384]{2,1,0:T(8,128)(2,1)} %ens_hbm.5), custom_call_target="tpu_custom_call" | custom-call | tf_op jit(solution)/shard_map/gram/pallas_call | solution.py:287
  36.3 23.8 %all_to_all.10.parts_ref = f32[32,40,128]{2,1,0:T(8,128)S(1)} all-to-all(f32[32,40,128]{2,1,0:T(8,128)S(1)} %gram.1), channel_id=1, replica_groups=mesh['tm'=8,'space'=32] {'space'}, dimensions={0} | all-to-all | bytes 1310720 | tf_op jit(solution)/shard_map/all_to_all | solution.py:304
  60.1 0.0 copy-done
  60.1 4.0 %transform.1 = (f32[2,64,64]{2,1,0:T(8,128)S(1)}, f32[64,64]{1,0:T(8,128)S(1)}) custom-call(f32[2]{0:T(128)S(1)} %copy-done, f32[32,40,128]{2,1,0:T(8,128)S(1)} %all_to_all.10.parts_ref), custom_call_target="tpu_custom_call" | custom-call | tf_op jit(solution)/shard_map/transform/pallas_call | solution.py:305
  64.2 0.1 collective-permute-start
  64.3 1.2 %collective-permute-done = f32[64,64]{1,0:T(8,128)S(1)} collective-permute-done((f32[64,64]{1,0:T(8,128)S(1)}, f32[64,64]{1,0:T(8,128)S(1)}, u32[]{:S(2)}, u32[]{:S(2)}) %collective-permute-start) | collective-permute-done | bytes 16416 | tf_op jit(solution)/shard_map/ppermute | solution.py:317
  65.4 0.2 fusion.5
  65.6 0.5 collective-permute-start.1
  66.1 3.5 %collective-permute-done.1 = f32[64,64]{1,0:T(8,128)S(1)} collective-permute-done((f32[64,64]{1,0:T(8,128)S(1)}, f32[64,64]{1,0:T(8,128)S(1)}, u32[]{:S(2)}, u32[]{:S(2)}) %collective-permute-start.1) | collective-permute-done | bytes 16416 | tf_op jit(solution)/shard_map/ppermute | solution.py:317
  69.6 0.2 fusion.2
  69.8 2.4 %collective-permute-start.2 = (f32[64,64]{1,0:T(8,128)S(1)}, f32[64,64]{1,0:T(8,128)S(1)}, u32[]{:S(2)}, u32[]{:S(2)}) collective-permute-start(f32[64,64]{1,0:T(8,128)S(1)} %fusion.2), channel_id=1, source_target_pairs={{0,128},{32,160},{64,192},{96,224},{128,0},{160,32},{192,64},{224,... | collective-permute-start | bytes 49160 | tf_op jit(solution)/shard_map/ppermute | solution.py:317
  72.2 0.2 fusion.1
  72.3 3.0 %collective-permute-done.2 = f32[64,64]{1,0:T(8,128)S(1)} collective-permute-done((f32[64,64]{1,0:T(8,128)S(1)}, f32[64,64]{1,0:T(8,128)S(1)}, u32[]{:S(2)}, u32[]{:S(2)}) %collective-permute-start.2) | collective-permute-done | bytes 16416 | tf_op jit(solution)/shard_map/ppermute | solution.py:317
  75.3 0.2 fusion.suffix_ref
  75.5 4.9 %apply.1 = f32[2,64,16384]{2,1,0:T(8,128)} custom-call(f32[64,64]{1,0:T(8,128)S(1)} %fusion.suffix_ref, f32[2,64,64]{2,1,0:T(8,128)S(1)} %get-tuple-element.8.made_ref, bf16[2,64,16384]{2,1,0:T(8,128)(2,1)} %ens_hbm.5), custom_call_target="tpu_custom_call" | custom-call | tf_op jit(solution)/shard_map/apply/pallas_call | solution.py:323
Async XLA Ops:
  0.0 60.1 %copy-start = (f32[2]{0:T(128)S(1)}, f32[2]{0:T(128)}, u32[]{:S(2)}) copy-start(f32[2]{0:T(128)} %infl_ref.1) | copy-start | bytes 28
  1.9 23.8 %all-to-all-start = ((f32[32,16,128]{2,1,0:T(8,128)}), f32[32,16,128]{2,1,0:T(8,128)S(1)}, u32[]{:S(2)}, u32[]{:S(2)}) async-start(f32[32,16,128]{2,1,0:T(8,128)} %route.1), calls=%async_computation | async-start | bytes 524288 | tf_op jit(solution)/shard_map/all_to_all | solution.py:276
  64.2 1.3 %collective-permute-start = (f32[64,64]{1,0:T(8,128)S(1)}, f32[64,64]{1,0:T(8,128)S(1)}, u32[]{:S(2)}, u32[]{:S(2)}) collective-permute-start(f32[64,64]{1,0:T(8,128)S(1)} %get-tuple-element.7), channel_id=1, source_target_pairs={{0,32},{32,0},{64,96},{96,64},{128,160},{160,128},{192,224},{224,1... | collective-permute-start | bytes 49160 | tf_op jit(solution)/shard_map/ppermute | solution.py:317
  65.6 4.0 %collective-permute-start.1 = (f32[64,64]{1,0:T(8,128)S(1)}, f32[64,64]{1,0:T(8,128)S(1)}, u32[]{:S(2)}, u32[]{:S(2)}) collective-permute-start(f32[64,64]{1,0:T(8,128)S(1)} %fusion.5), channel_id=1, source_target_pairs={{0,64},{32,96},{64,0},{96,32},{128,192},{160,224},{192,128},{224,1... | collective-permute-start | bytes 49160 | tf_op jit(solution)/shard_map/ppermute | solution.py:317
  69.8 5.5 %collective-permute-start.2 = (f32[64,64]{1,0:T(8,128)S(1)}, f32[64,64]{1,0:T(8,128)S(1)}, u32[]{:S(2)}, u32[]{:S(2)}) collective-permute-start(f32[64,64]{1,0:T(8,128)S(1)} %fusion.2), channel_id=1, source_target_pairs={{0,128},{32,160},{64,192},{96,224},{128,0},{160,32},{192,64},{224,... | collective-permute-start | bytes 49160 | tf_op jit(solution)/shard_map/ppermute | solution.py:317

commit v2 on v1

v2 whole, which is shorter than its diff:
```python
import math

import jax
import jax.numpy as jnp
from jax import lax
from jax.experimental import pallas as pl
from jax.experimental.pallas import tpu as pltpu
from jax.sharding import PartitionSpec as P

MEMB = 64
BLOCK = 256
SLOTS = 32
SHARDS = 32
NBLK = 64
CELLS = NBLK * BLOCK
HALF = MEMB // 2
STEP = 8
WIDTH = 4096

f32 = jnp.float32
bf16 = jnp.bfloat16
exact_mode = lax.Precision.HIGHEST
NT = (((1,), (1,)), ((), ()))


def iota(shape, dim):
    return lax.broadcasted_iota(jnp.int32, shape, dim)


def split(x):
    hi = x.astype(bf16)
    return hi, (x - hi.astype(f32)).astype(bf16)


def route_kernel(owner_ref, local_ref, offset_ref, count_ref, value_ref, var_ref, out_ref):
    for w in range(2):
        owner = owner_ref[w : w + 1, :]
        across = jnp.broadcast_to(owner, (128, 128))
        same = jnp.where((across == across.T) & (iota((128, 128), 0) < iota((128, 128), 1)), 1.0, 0.0)
        rank = jnp.sum(same, axis=0, keepdims=True).astype(jnp.int32)
        target = owner * 2 + rank // 4
        placer = jnp.where(iota((2 * SHARDS, 128), 0) == target, 1.0, 0.0).astype(bf16)
        live = iota((SLOTS, 128), 0) < count_ref[w : w + 1, :]
        precision = jnp.where(live, 1.0 / var_ref[w], 0.0)
        rows = jnp.concatenate(
            [precision, precision * value_ref[w], (local_ref[w : w + 1, :] * BLOCK + offset_ref[w]).astype(f32)],
            axis=0,
        )
        wide = jnp.concatenate(
            [
                jnp.where(rank % 4 == c, rows[SLOTS * q : SLOTS * q + SLOTS], 0.0)
                for q in range(3)
                for c in range(4)
            ],
            axis=0,
        )
        high = wide.astype(bf16)
        rest = wide - high.astype(f32)
        middle = rest.astype(bf16)
        low = (rest - middle.astype(f32)).astype(bf16)
        placed = sum(
            lax.dot_general(placer, part, NT, preferred_element_type=f32) for part in (low, middle, high)
        )
        for q in range(3):
            out_ref[:, q, 2 * w : 2 * w + 2, :] = placed[:, 128 * q : 128 * q + 128].reshape(SHARDS, 2, 128)


def center_kernel(ens_hbm, mean_ref, ens, sems):
    copies = [
        pltpu.make_async_copy(
            ens_hbm.at[i // 4, :, pl.ds(i % 4 * 4096, 4096)], ens.at[i // 4, :, pl.ds(i % 4 * 4096, 4096)], sems.at[i]
        )
        for i in range(8)
    ]
    for copy in copies:
        copy.start()
    for i in range(8):
        copies[i].wait()

        def some(step, carry):
            block = i % 4 * 16 + step * 8
            for k in range(8):
                where = pl.ds(pl.multiple_of((block + k) * BLOCK, BLOCK), BLOCK)
                members = ens[i // 4, :, where].astype(f32)
                mean_ref[i // 4, pl.ds(block + k, 1), :] = jnp.sum(members, axis=0, keepdims=True) * (1.0 / MEMB)
            return carry

        lax.fori_loop(0, 2, some, 0)


def gram_kernel(recv_ref, mean_ref, ens_hbm, out_ref, ens, sems, table, dense, scale, ratio, even, odd, sums):
    copies = [pltpu.make_async_copy(ens_hbm.at[w], ens.at[w], sems.at[w]) for w in range(2)]
    for copy in copies:
        copy.start()
    for q in range(3):
        table[q] = jnp.concatenate(
            [recv_ref[:, q, 2 * w : 2 * w + 2, :].reshape(2 * SHARDS, 128) for w in range(2)], axis=0
        ).T
    locals_ = []
    for c in range(4):
        held = jnp.floor(table[2, SLOTS * c : SLOTS * c + 1, :] * (1.0 / BLOCK))
        locals_.append(held)
        table[2, SLOTS * c : SLOTS * c + SLOTS, :] = table[2, SLOTS * c : SLOTS * c + SLOTS, :] - held * BLOCK

    def scatter(tile, carry):
        base = pl.multiple_of(tile * 32, 32)
        cells = (iota((32, 128), 0) + base).astype(f32)
        for c in range(4):
            acc_u = jnp.zeros((32, 128), f32)
            acc_t = jnp.zeros((32, 128), f32)
            for r in range(SLOTS * c, SLOTS * c + SLOTS):
                hit = table[2, r : r + 1, :] == cells
                acc_u += jnp.where(hit, table[0, r : r + 1, :], 0.0)
                acc_t += jnp.where(hit, table[1, r : r + 1, :], 0.0)
            dense[pl.ds(base, 32), 128 * c : 128 * c + 128] = acc_u
            dense[pl.ds(base + 256, 32), 128 * c : 128 * c + 128] = acc_t
        return carry

    lax.fori_loop(0, 8, scatter, 0)
    row, lane = iota((2 * NBLK, 128), 0), iota((2 * NBLK, 128), 1)
    ours = (row // NBLK) == (lane // NBLK)
    holder = jnp.concatenate(
        [jnp.where(ours & ((row % NBLK).astype(f32) == held), 1.0, 0.0) for held in locals_], axis=1
    ).astype(bf16)
    placed = sum(lax.dot_general(holder, part, NT, preferred_element_type=f32) for part in split(dense[...])[::-1])
    for w in range(2):
        total = placed[NBLK * w : NBLK * w + NBLK, :256]
        root = jnp.sqrt(total)
        scale[w] = root
        ratio[w] = jnp.where(
            total > 0.0, (placed[NBLK * w : NBLK * w + NBLK, 256:] - total * mean_ref[w]) / root, 0.0
        )
    row16 = iota((16, BLOCK), 0)

    def fill(ref, step):
        w = step // 8
        for k in range(8):
            b = step % 8 * 8 + k
            here = slice(BLOCK * k, BLOCK * k + BLOCK)
            cells = ens[w, :, pl.ds(pl.multiple_of(b * BLOCK, BLOCK), BLOCK)].astype(f32)
            high, low = split((cells - mean_ref[w, pl.ds(b, 1), :]) * scale[w, pl.ds(b, 1), :])
            ref[16 : 16 + MEMB, here] = high
            ref[16 + MEMB :, here] = low
            extra = ratio[w, pl.ds(b, 1), :]
            top = extra.astype(bf16).astype(f32)
            ref[0:16, here] = jnp.where(row16 == 0, top, jnp.where(row16 == 1, extra - top, 0.0)).astype(bf16)

    def product(ref, step):
        w = step // 8
        sums[w] = sums[w] + lax.dot_general(ref[16:, :], ref[: MEMB + 16, :], NT, preferred_element_type=f32)

    def steps(i, carry):
        product(even, 2 * i)
        fill(odd, 2 * i + 1)
        product(odd, 2 * i + 1)
        fill(even, jnp.minimum(2 * i + 2, 15))
        return carry

    sums[...] = jnp.zeros((2, 2 * MEMB, MEMB + 16), f32)
    for copy in copies:
        copy.wait()
    fill(even, 0)
    lax.fori_loop(0, 8, steps, 0)
    row, col = iota((MEMB, MEMB), 0), iota((MEMB, MEMB), 1)
    lines = []
    for w in range(2):
        full = sums[w]
        cross = full[MEMB:, 16:]
        gram = full[:MEMB, 16:] + (cross + cross.T)
        both = full[:MEMB] + full[MEMB:]
        proj = jnp.sum(jnp.where(row == col, both[:, :1] + both[:, 1:2], 0.0), axis=0, keepdims=True)
        diag = jnp.sum(jnp.where(row == col, gram, 0.0), axis=0, keepdims=True)
        mixed = jnp.where(row[:HALF, :HALF] <= col[:HALF, :HALF], gram[:HALF, :HALF], gram[HALF:, HALF:])
        halves = jnp.concatenate([mixed, gram[:HALF, HALF:]], axis=1)
        body = jnp.concatenate([halves[:16], halves[16:]], axis=1)
        last = jnp.concatenate([proj, diag], axis=1)
        lines.append(jnp.concatenate([body[r : r + 1] for r in range(16)] + [last], axis=1))
    for d in range(SHARDS):
        out_ref[d] = lines[d % 2]


def eliminate(systems):
    row, lane = iota((MEMB, 2 * MEMB), 0), iota((MEMB, 2 * MEMB), 1)
    eye = jnp.where(row + MEMB == lane, 1.0, 0.0)
    count = len(systems)
    tiles = []
    for system in systems:
        wide = jnp.concatenate([system, jnp.zeros((MEMB, MEMB), f32)], axis=1) + eye
        tiles.append([wide[8 * i : 8 * i + 8] for i in range(MEMB // 8)])
    found = [[] for _ in systems]
    full = (8, 2 * MEMB)
    for j in range(0, MEMB, STEP):
        t, s = divmod(j, 8)
        for w in range(count):
            rows = [jnp.broadcast_to(tiles[w][t][s + k : s + k + 1, :], full) for k in range(STEP)]
            block = [
                [jnp.broadcast_to(rows[k][:, j + l : j + l + 1], full) if l >= k else None for l in range(STEP)]
                for k in range(STEP)
            ]
            inverses, lower = [], [[None] * STEP for _ in range(STEP)]
            for k in range(STEP):
                inv = 1.0 / block[k][k]
                inverses.append(inv)
                for l in range(k + 1, STEP):
                    lower[l][k] = block[k][l] * inv
                for l in range(k + 1, STEP):
                    for m in range(l, STEP):
                        block[l][m] = block[l][m] - lower[l][k] * block[k][m]
                    rows[l] = rows[l] - lower[l][k] * rows[k]
            for k in range(STEP):
                found[w].append(rows[k][:1, :] * lax.rsqrt(block[k][k][:1, :]))
            first = t if s + STEP < 8 else t + 1
            if first == MEMB // 8:
                continue
            solved = [None] * STEP
            for k in reversed(range(STEP)):
                value = rows[k] * inverses[k]
                for l in range(k + 1, STEP):
                    value = value - lower[l][k] * solved[l]
                solved[k] = value
            for i in range(first, MEMB // 8):
                tile = tiles[w][i]
                change = None
                for k in range(STEP):
                    part = jnp.broadcast_to(tile[:, j + k : j + k + 1], full) * solved[k]
                    change = part if change is None else change + part
                tiles[w][i] = tile - change
    return [jnp.concatenate(rows, axis=0)[:, MEMB:] for rows in found]


def transform_kernel(infl_ref, parts_ref, out_ref):
    total = jnp.sum(parts_ref[...], axis=0)
    body = jnp.concatenate([total[:, 128 * r : 128 * r + 128] for r in range(16)], axis=0)
    proj = total[:, 2048 : 2048 + MEMB]
    halves = jnp.concatenate([body[:, :MEMB], body[:, MEMB:]], axis=0)
    mixed, corner = halves[:, :HALF], halves[:, HALF:]
    other = mixed.T
    row, col = iota((HALF, HALF), 0), iota((HALF, HALF), 1)
    diag = jnp.where(row == col, total[:, 2048 + MEMB + HALF : 2048 + 2 * MEMB], 0.0)
    upper = jnp.where(row <= col, mixed, other)
    under = jnp.where(row > col, mixed, jnp.where(row < col, other, diag))
    gram = jnp.concatenate(
        [jnp.concatenate([upper, corner], axis=1), jnp.concatenate([corner.T, under], axis=1)], axis=0
    )
    ridge = jnp.where(iota((MEMB, MEMB), 0) == iota((MEMB, MEMB), 1), MEMB - 1.0, 0.0)
    inverse = eliminate([gram + ridge])[0]
    half = jnp.sum(inverse * proj, axis=1, keepdims=True)
    weight = jnp.sum(inverse * half, axis=0, keepdims=True)
    inner = weight + (infl_ref[0] * math.sqrt(MEMB - 1.0)) * inverse
    out_ref[...] = 1.0 / MEMB + inner - jnp.sum(inner, axis=1, keepdims=True) * (1.0 / MEMB)


def exact(a, b):
    return jnp.dot(a, b, precision=exact_mode, preferred_element_type=f32)


def apply_kernel(suffix_ref, first_ref, second_ref, ens_hbm, out_hbm, ens, out, in_sems, out_sems):
    pieces = 16384 // WIDTH

    def part(i):
        return (i // pieces, slice(None), pl.ds(i % pieces * WIDTH, WIDTH))

    reads = [pltpu.make_async_copy(ens_hbm.at[part(i)], ens.at[i], in_sems.at[i]) for i in range(2 * pieces)]
    for copy in reads:
        copy.start()
    last = exact(suffix_ref[...], second_ref[...])
    totals = [exact(last, first_ref[...]), last]
    writes = []
    for i in range(2 * pieces):
        reads[i].wait()
        both = jnp.concatenate(split(totals[i // pieces]), axis=1)
        cells = ens[i]
        out[i] = jnp.dot(both, jnp.concatenate([cells, cells], axis=0), preferred_element_type=f32)
        writes.append(pltpu.make_async_copy(out.at[i], out_hbm.at[part(i)], out_sems.at[i]))
        writes[i].start()
    for copy in writes:
        copy.wait()


def times(a, b):
    return jnp.matmul(a, b, precision=exact_mode)


def body(ensemble, obs_owner, obs_local, obs_offset, obs_count, obs_value, obs_var, inflation):
    vmem = pl.BlockSpec(memory_space=pltpu.VMEM)
    turned = lambda a: jnp.swapaxes(a, 1, 2)
    routed = pl.pallas_call(
        route_kernel,
        out_shape=pltpu.VMEM((SHARDS, 3, 4, 128), f32),
        in_specs=[vmem] * 6,
        out_specs=vmem,
        name="route",
    )(obs_owner[:, :, 0], obs_local, turned(obs_offset), obs_count, turned(obs_value), turned(obs_var))
    recv = lax.all_to_all(routed, "space", split_axis=0, concat_axis=0, tiled=True)
    ensemble = pltpu.with_memory_space_constraint(ensemble, pltpu.HBM)
    means = pl.pallas_call(
        center_kernel,
        out_shape=pltpu.VMEM((2, NBLK, BLOCK), f32),
        in_specs=[pl.BlockSpec(memory_space=pl.ANY)],
        out_specs=vmem,
        scratch_shapes=[pltpu.VMEM((2, MEMB, CELLS), bf16), pltpu.SemaphoreType.DMA((8,))],
        compiler_params=pltpu.CompilerParams(vmem_limit_bytes=20 * 2**20),
        name="center",
    )(ensemble)
    partial = pl.pallas_call(
        gram_kernel,
        out_shape=pltpu.VMEM((SHARDS, 1, 2176), f32),
        in_specs=[vmem, vmem, pl.BlockSpec(memory_space=pl.ANY)],
        out_specs=vmem,
        scratch_shapes=[
            pltpu.VMEM((2, MEMB, CELLS), bf16),
            pltpu.SemaphoreType.DMA((2,)),
            pltpu.VMEM((3, 128, 128), f32),
            pltpu.VMEM((512, 512), f32),
            pltpu.VMEM((2, NBLK, BLOCK), f32),
            pltpu.VMEM((2, NBLK, BLOCK), f32),
            pltpu.VMEM((2 * MEMB + 16, 8 * BLOCK), bf16),
            pltpu.VMEM((2 * MEMB + 16, 8 * BLOCK), bf16),
            pltpu.VMEM((2, 2 * MEMB, MEMB + 16), f32),
        ],
        compiler_params=pltpu.CompilerParams(vmem_limit_bytes=30 * 2**20),
        name="gram",
    )(recv, means, ensemble)
    parts = lax.all_to_all(partial, "space", split_axis=0, concat_axis=0, tiled=True)
    second = (lax.axis_index("space") & 1) == 1
    made = pl.pallas_call(
        transform_kernel,
        out_shape=pltpu.VMEM((MEMB, MEMB), f32),
        in_specs=[pl.BlockSpec(memory_space=pltpu.SMEM), vmem],
        out_specs=vmem,
        compiler_params=pltpu.CompilerParams(vmem_limit_bytes=20 * 2**20),
        name="transform",
    )(jnp.where(second, inflation[1:], inflation[:1]), parts)
    paired = lax.ppermute(made, "space", [(i, i ^ 1) for i in range(SHARDS)])
    early, late = jnp.where(second, paired, made), jnp.where(second, made, paired)
    product = times(late, early)
    place = lax.axis_index("tm")
    eye = jnp.eye(MEMB, dtype=f32)
    suffix = eye
    for bit in (1, 2, 4):
        other = lax.ppermute(product, "tm", [(i, i ^ bit) for i in range(8)])
        first = (place & bit) == 0
        ahead = jnp.where(first, other, eye)
        suffix = ahead if bit == 1 else times(ahead, suffix)
        if bit < 4:
            product = times(jnp.where(first, other, product), jnp.where(first, product, other))
    return pl.pallas_call(
        apply_kernel,
        out_shape=jax.ShapeDtypeStruct((2, MEMB, CELLS), f32),
        in_specs=[vmem, vmem, vmem, pl.BlockSpec(memory_space=pl.ANY)],
        out_specs=pl.BlockSpec(memory_space=pl.ANY),
        scratch_shapes=[
            pltpu.VMEM((2 * CELLS // WIDTH, MEMB, WIDTH), bf16),
            pltpu.VMEM((2 * CELLS // WIDTH, MEMB, WIDTH), f32),
            pltpu.SemaphoreType.DMA((2 * CELLS // WIDTH,)),
            pltpu.SemaphoreType.DMA((2 * CELLS // WIDTH,)),
        ],
        compiler_params=pltpu.CompilerParams(vmem_limit_bytes=30 * 2**20),
        name="apply",
    )(suffix, early, late, ensemble)


def solution(mesh):
    in_specs = (
        P("tm", None, "space"),
        P("tm", "space", None),
        P("tm", "space"),
        P("tm", "space", None),
        P("tm", "space"),
        P("tm", "space", None),
        P("tm", "space", None),
        P("tm"),
    )
    out_specs = P("tm", None, "space")
    return jax.shard_map(body, mesh=mesh, in_specs=in_specs, out_specs=out_specs, check_vma=False)
```

time: 80.6 us -> 73.4 us (0.911)
  blocking collectives: 23.8 us -> 0 us
  waiting for transfers between devices: 17.7 us -> 28.8 us
  starting transfers between devices: 14.3 us -> 20.3 us
  Pallas kernels: 23.8 us -> 21.2 us
  between operations: 0.09 us -> 1.37 us
    all_to_all x1 -> x0, blocking collectives: 23.8 us -> none  [body(): lax.all_to_all(partial, 'space', split_axis=0, concat_axis=0, tiled=True)]
    all_to_all x0 -> x1, waiting for transfers between devices: none -> 10.1 us  [body(): lax.all_to_all(partial, 'space', split_axis=0, concat_axis=0, tiled=True)]
    all_to_all x0 -> x1, starting transfers between devices: none -> 4.15 us  [body(): lax.all_to_all(partial, 'space', split_axis=0, concat_axis=0, tiled=True)]
    pallas_call x3, Pallas kernels: 16.5 us -> 13.9 us  [the longest x1 8.77 us: body(): pl.pallas_call(gram_kernel, out_shape=pltpu.VMEM((SHARDS, 1, 2176), f32),...]
    ppermute x0 -> x1, waiting for transfers between devices: none -> 2.09 us  [body(): paired = lax.ppermute(made, 'space', [(i, i ^ 1) for i in range(SHARDS)])]
    ppermute x0 -> x1, starting transfers between devices: none -> 1.87 us  [body(): paired = lax.ppermute(made, 'space', [(i, i ^ 1) for i in range(SHARDS)])]
    all_to_all x1, waiting for transfers between devices: 10.1 us -> 8.96 us  [body(): lax.all_to_all(routed, 'space', split_axis=0, concat_axis=0, tiled=True)]
  transfers between devices with their start and end apart: 4 -> 6, of which waited for: 4 -> 6; matrix products, arithmetic and copies ran while one was open for 0% -> 1% of each run, Pallas kernels for 3% -> 3%
where the time goes in v2:
time: 73.4 us; the launch traced here: 73.1 us
  waiting for transfers between devices  28.8 us (39%)
  Pallas kernels  21.2 us (29%)
  starting transfers between devices  20.3 us (28%)
  between operations  1.37 us (2%)
  matrix products  0.81 us (1%)
    all_to_all x1, starting transfers between devices, body(): lax.all_to_all(routed, 'space', split_axis=0, concat_axis=0, tiled=True)  11.3 us
    all_to_all x1, waiting for transfers between devices, body(): lax.all_to_all(partial, 'space', split_axis=0, concat_axis=0, tiled=True)  10.1 us
    all_to_all x1, waiting for transfers between devices, body(): lax.all_to_all(routed, 'space', split_axis=0, concat_axis=0, tiled=True)  8.96 us
    pallas_call x1, Pallas kernels, body(): pl.pallas_call(gram_kernel, out_shape=pltpu.VMEM((SHARDS, 1, 2176), f32),...  8.77 us
    ppermute x3, waiting for transfers between devices, body(): other = lax.ppermute(product, 'tm', [(i, i ^ bit) for i in range(8)])  7.61 us
    pallas_call x1, Pallas kernels, body(): pl.pallas_call(apply_kernel, out_shape=jax.ShapeDtypeStruct((2, MEMB, CEL...  4.88 us
    all_to_all x1, starting transfers between devices, body(): lax.all_to_all(partial, 'space', split_axis=0, concat_axis=0, tiled=True)  4.15 us
    pallas_call x1, Pallas kernels, body(): pl.pallas_call(transform_kernel, out_shape=pltpu.VMEM((MEMB, MEMB), f32),...  3.12 us
  transfers between devices with their start and end apart: 6, of which 6 were waited for; matrix products, arithmetic and copies ran while one was open for 1% of the time, Pallas kernels for 3%

profile of v2, /device:TPU:8, one launch (start us, length us, event | category | flops | bytes accessed | tf_op | source)
XLA Modules:
  0.0 73.1 jit_solution(2239721534234942636)
XLA Ops:
  0.0 0.0 copy-start
  0.0 2.1 %route.1 = f32[32,3,4,128]{3,2,1,0:T(4,128)} custom-call(s32[2,128]{1,0:T(2,128)} %bitcast.11, s32[2,128]{1,0:T(2,128)} %local_ref.1, s32[2,32,128]{2,1,0:T(8,128)} %bitcast.8, s32[2,128]{1,0:T(2,128)} %count_ref.1, f32[2,32,128]{2,1,0:T(8,128)} %bitcast.9, f32[2,32,128]{2,1,0:T(8,128)} %bitcast.10), custom_call_target="tpu_custom_call" | custom-call | tf_op jit(solution)/shard_map/route/pallas_call | solution.py:287
  2.1 11.3 %all-to-all-start = ((f32[32,3,4,128]{3,2,1,0:T(4,128)}), f32[32,3,4,128]{3,2,1,0:T(4,128)S(1)}, u32[]{:S(2)}, u32[]{:S(2)}) async-start(f32[32,3,4,128]{3,2,1,0:T(4,128)} %route.1), calls=%async_computation | async-start | bytes 393216 | tf_op jit(solution)/shard_map/all_to_all | solution.py:294
  13.4 2.3 %center.1.mean_ref = f32[2,64,256]{2,1,0:T(8,128)S(1)} custom-call(bf16[2,64,16384]{2,1,0:T(8,128)(2,1)} %ens_hbm.5), custom_call_target="tpu_custom_call" | custom-call | tf_op jit(solution)/shard_map/center/pallas_call | solution.py:296
  15.7 9.0 %all-to-all-done.recv_ref = f32[32,3,4,128]{3,2,1,0:T(4,128)S(1)} async-done(((f32[32,3,4,128]{3,2,1,0:T(4,128)}), f32[32,3,4,128]{3,2,1,0:T(4,128)S(1)}, u32[]{:S(2)}, u32[]{:S(2)}) %all-to-all-start) | async-done | bytes 196640 | tf_op jit(solution)/shard_map/all_to_all | solution.py:294
  24.7 8.8 %gram.1 = f32[32,1,2176]{2,1,0:T(1,128)} custom-call(f32[32,3,4,128]{3,2,1,0:T(4,128)S(1)} %all-to-all-done.recv_ref, f32[2,64,256]{2,1,0:T(8,128)S(1)} %center.1.mean_ref, bf16[2,64,16384]{2,1,0:T(8,128)(2,1)} %ens_hbm.5), custom_call_target="tpu_custom_call" | custom-call | tf_op jit(solution)/shard_map/gram/pallas_call | solution.py:305
  33.5 4.1 %all-to-all-start.1 = ((f32[32,1,2176]{2,1,0:T(1,128)}), f32[32,1,2176]{2,1,0:T(1,128)S(1)}, u32[]{:S(2)}, u32[]{:S(2)}) async-start(f32[32,1,2176]{2,1,0:T(1,128)} %gram.1), calls=%async_computation.1 | async-start | bytes 557056 | tf_op jit(solution)/shard_map/all_to_all | solution.py:324
  37.6 0.0 copy-done
  37.6 0.6 fusion.13
  39.5 10.1 %all-to-all-done.1.parts_ref = f32[32,1,2176]{2,1,0:T(1,128)S(1)} async-done(((f32[32,1,2176]{2,1,0:T(1,128)}), f32[32,1,2176]{2,1,0:T(1,128)S(1)}, u32[]{:S(2)}, u32[]{:S(2)}) %all-to-all-start.1) | async-done | bytes 278560 | tf_op jit(solution)/shard_map/all_to_all | solution.py:324
  49.6 3.1 %transform.1 = f32[64,64]{1,0:T(8,128)S(1)} custom-call(f32[1]{0:T(128)S(6)} %select_n.61.infl_ref, f32[32,1,2176]{2,1,0:T(1,128)S(1)} %all-to-all-done.1.parts_ref), custom_call_target="tpu_custom_call" | custom-call | tf_op jit(solution)/shard_map/transform/pallas_call | solution.py:326
  52.7 1.9 %collective-permute-start = (f32[64,64]{1,0:T(8,128)S(1)}, f32[64,64]{1,0:T(8,128)S(1)}, u32[]{:S(2)}, u32[]{:S(2)}) collective-permute-start(f32[64,64]{1,0:T(8,128)S(1)} %transform.1), channel_id=1, source_target_pairs={{0,1},{1,0},{2,3},{3,2},{4,5},{5,4},{6,7},{7,6},{8,9},{9,8},{10,11... | collective-permute-start | bytes 49160 | tf_op jit(solution)/shard_map/ppermute | solution.py:334
  54.6 2.1 %collective-permute-done = f32[64,64]{1,0:T(8,128)S(1)} collective-permute-done((f32[64,64]{1,0:T(8,128)S(1)}, f32[64,64]{1,0:T(8,128)S(1)}, u32[]{:S(2)}, u32[]{:S(2)}) %collective-permute-start) | collective-permute-done | bytes 16416 | tf_op jit(solution)/shard_map/ppermute | solution.py:334
  56.7 0.2 fusion.14
  56.9 0.1 collective-permute-start.1
  57.0 1.2 %collective-permute-done.1 = f32[64,64]{1,0:T(8,128)S(1)} collective-permute-done((f32[64,64]{1,0:T(8,128)S(1)}, f32[64,64]{1,0:T(8,128)S(1)}, u32[]{:S(2)}, u32[]{:S(2)}) %collective-permute-start.1) | collective-permute-done | bytes 16416 | tf_op jit(solution)/shard_map/ppermute | solution.py:341
  58.2 0.2 fusion.5
  58.3 0.5 collective-permute-start.2
  58.9 3.5 %collective-permute-done.2 = f32[64,64]{1,0:T(8,128)S(1)} collective-permute-done((f32[64,64]{1,0:T(8,128)S(1)}, f32[64,64]{1,0:T(8,128)S(1)}, u32[]{:S(2)}, u32[]{:S(2)}) %collective-permute-start.2) | collective-permute-done | bytes 16416 | tf_op jit(solution)/shard_map/ppermute | solution.py:341
  62.3 0.2 fusion.2
  62.5 2.4 %collective-permute-start.3 = (f32[64,64]{1,0:T(8,128)S(1)}, f32[64,64]{1,0:T(8,128)S(1)}, u32[]{:S(2)}, u32[]{:S(2)}) collective-permute-start(f32[64,64]{1,0:T(8,128)S(1)} %fusion.2), channel_id=1, source_target_pairs={{0,128},{32,160},{64,192},{96,224},{128,0},{160,32},{192,64},{224,... | collective-permute-start | bytes 49160 | tf_op jit(solution)/shard_map/ppermute | solution.py:341
  64.9 0.2 fusion.1
  65.0 3.0 %collective-permute-done.3 = f32[64,64]{1,0:T(8,128)S(1)} collective-permute-done((f32[64,64]{1,0:T(8,128)S(1)}, f32[64,64]{1,0:T(8,128)S(1)}, u32[]{:S(2)}, u32[]{:S(2)}) %collective-permute-start.3) | collective-permute-done | bytes 16416 | tf_op jit(solution)/shard_map/ppermute | solution.py:341
  68.0 0.2 fusion.suffix_ref
  68.2 4.9 %apply.1 = f32[2,64,16384]{2,1,0:T(8,128)} custom-call(f32[64,64]{1,0:T(8,128)S(1)} %fusion.suffix_ref, f32[64,64]{1,0:T(8,128)S(1)} %get-tuple-element.5.first_ref, f32[64,64]{1,0:T(8,128)S(1)} %get-tuple-element.6.second_ref, bf16[2,64,16384]{2,1,0:T(8,128)(2,1)} %ens_hbm.5), custom_call_target="tpu_custom_call" | custom-call | tf_op jit(solution)/shard_map/apply/pallas_call | solution.py:347
  (1 shorter events, 0.0 us)
Async XLA Ops:
  0.0 37.6 %copy-start = (f32[2]{0:T(128)S(1)}, f32[2]{0:T(128)}, u32[]{:S(2)}) copy-start(f32[2]{0:T(128)} %param.15) | copy-start | bytes 28
  2.1 22.6 %all-to-all-start = ((f32[32,3,4,128]{3,2,1,0:T(4,128)}), f32[32,3,4,128]{3,2,1,0:T(4,128)S(1)}, u32[]{:S(2)}, u32[]{:S(2)}) async-start(f32[32,3,4,128]{3,2,1,0:T(4,128)} %route.1), calls=%async_computation | async-start | bytes 393216 | tf_op jit(solution)/shard_map/all_to_all | solution.py:294
  33.5 16.1 %all-to-all-start.1 = ((f32[32,1,2176]{2,1,0:T(1,128)}), f32[32,1,2176]{2,1,0:T(1,128)S(1)}, u32[]{:S(2)}, u32[]{:S(2)}) async-start(f32[32,1,2176]{2,1,0:T(1,128)} %gram.1), calls=%async_computation.1 | async-start | bytes 557056 | tf_op jit(solution)/shard_map/all_to_all | solution.py:324
  52.7 4.0 %collective-permute-start = (f32[64,64]{1,0:T(8,128)S(1)}, f32[64,64]{1,0:T(8,128)S(1)}, u32[]{:S(2)}, u32[]{:S(2)}) collective-permute-start(f32[64,64]{1,0:T(8,128)S(1)} %transform.1), channel_id=1, source_target_pairs={{0,1},{1,0},{2,3},{3,2},{4,5},{5,4},{6,7},{7,6},{8,9},{9,8},{10,11... | collective-permute-start | bytes 49160 | tf_op jit(solution)/shard_map/ppermute | solution.py:334
  56.9 1.3 %collective-permute-start.1 = (f32[64,64]{1,0:T(8,128)S(1)}, f32[64,64]{1,0:T(8,128)S(1)}, u32[]{:S(2)}, u32[]{:S(2)}) collective-permute-start(f32[64,64]{1,0:T(8,128)S(1)} %fusion.14), channel_id=1, source_target_pairs={{0,32},{32,0},{64,96},{96,64},{128,160},{160,128},{192,224},{224,1... | collective-permute-start | bytes 49160 | tf_op jit(solution)/shard_map/ppermute | solution.py:341
  58.3 4.0 %collective-permute-start.2 = (f32[64,64]{1,0:T(8,128)S(1)}, f32[64,64]{1,0:T(8,128)S(1)}, u32[]{:S(2)}, u32[]{:S(2)}) collective-permute-start(f32[64,64]{1,0:T(8,128)S(1)} %fusion.5), channel_id=1, source_target_pairs={{0,64},{32,96},{64,0},{96,32},{128,192},{160,224},{192,128},{224,1... | collective-permute-start | bytes 49160 | tf_op jit(solution)/shard_map/ppermute | solution.py:341
  62.5 5.5 %collective-permute-start.3 = (f32[64,64]{1,0:T(8,128)S(1)}, f32[64,64]{1,0:T(8,128)S(1)}, u32[]{:S(2)}, u32[]{:S(2)}) collective-permute-start(f32[64,64]{1,0:T(8,128)S(1)} %fusion.2), channel_id=1, source_target_pairs={{0,128},{32,160},{64,192},{96,224},{128,0},{160,32},{192,64},{224,... | collective-permute-start | bytes 49160 | tf_op jit(solution)/shard_map/ppermute | solution.py:341

commit v3 on v2

--- a/solution.py
+++ b/solution.py
@@ -13,7 +13,10 @@
 SHARDS = 32
 NBLK = 64
 CELLS = NBLK * BLOCK
+CHUNKS = 16
+PER = NBLK // CHUNKS
 HALF = MEMB // 2
+LINE = 9
 STEP = 8
 WIDTH = 4096
 
@@ -133,9 +136,9 @@
     row16 = iota((16, BLOCK), 0)
 
     def fill(ref, step):
-        w = step // 8
-        for k in range(8):
-            b = step % 8 * 8 + k
+        w = step // PER
+        for k in range(CHUNKS):
+            b = step % PER * CHUNKS + k
             here = slice(BLOCK * k, BLOCK * k + BLOCK)
             cells = ens[w, :, pl.ds(pl.multiple_of(b * BLOCK, BLOCK), BLOCK)].astype(f32)
             high, low = split((cells - mean_ref[w, pl.ds(b, 1), :]) * scale[w, pl.ds(b, 1), :])
@@ -146,21 +149,21 @@
             ref[0:16, here] = jnp.where(row16 == 0, top, jnp.where(row16 == 1, extra - top, 0.0)).astype(bf16)
 
     def product(ref, step):
-        w = step // 8
+        w = step // PER
         sums[w] = sums[w] + lax.dot_general(ref[16:, :], ref[: MEMB + 16, :], NT, preferred_element_type=f32)
 
     def steps(i, carry):
         product(even, 2 * i)
         fill(odd, 2 * i + 1)
         product(odd, 2 * i + 1)
-        fill(even, jnp.minimum(2 * i + 2, 15))
+        fill(even, jnp.minimum(2 * i + 2, 2 * PER - 1))
         return carry
 
     sums[...] = jnp.zeros((2, 2 * MEMB, MEMB + 16), f32)
     for copy in copies:
         copy.wait()
     fill(even, 0)
-    lax.fori_loop(0, 8, steps, 0)
+    lax.fori_loop(0, PER, steps, 0)
     row, col = iota((MEMB, MEMB), 0), iota((MEMB, MEMB), 1)
     lines = []
     for w in range(2):
@@ -174,7 +177,10 @@
         halves = jnp.concatenate([mixed, gram[:HALF, HALF:]], axis=1)
         body = jnp.concatenate([halves[:16], halves[16:]], axis=1)
         last = jnp.concatenate([proj, diag], axis=1)
-        lines.append(jnp.concatenate([body[r : r + 1] for r in range(16)] + [last], axis=1))
+        rows = [body[r : r + 1] for r in range(16)] + [last, jnp.zeros((1, 128), f32)]
+        lines.append(
+            jnp.concatenate([jnp.concatenate([rows[r], rows[r + LINE]], axis=0) for r in range(LINE)], axis=1)
+        )
     for d in range(SHARDS):
         out_ref[d] = lines[d % 2]
 
@@ -230,13 +236,14 @@
 
 def transform_kernel(infl_ref, parts_ref, out_ref):
     total = jnp.sum(parts_ref[...], axis=0)
-    body = jnp.concatenate([total[:, 128 * r : 128 * r + 128] for r in range(16)], axis=0)
-    proj = total[:, 2048 : 2048 + MEMB]
+    rows = [total[p : p + 1, 128 * r : 128 * r + 128] for p in range(2) for r in range(LINE)]
+    body = jnp.concatenate(rows[:16], axis=0)
+    proj = rows[16][:, :MEMB]
     halves = jnp.concatenate([body[:, :MEMB], body[:, MEMB:]], axis=0)
     mixed, corner = halves[:, :HALF], halves[:, HALF:]
     other = mixed.T
     row, col = iota((HALF, HALF), 0), iota((HALF, HALF), 1)
-    diag = jnp.where(row == col, total[:, 2048 + MEMB + HALF : 2048 + 2 * MEMB], 0.0)
+    diag = jnp.where(row == col, rows[16][:, MEMB + HALF :], 0.0)
     upper = jnp.where(row <= col, mixed, other)
     under = jnp.where(row > col, mixed, jnp.where(row < col, other, diag))
     gram = jnp.concatenate(
@@ -246,7 +253,7 @@
     inverse = eliminate([gram + ridge])[0]
     half = jnp.sum(inverse * proj, axis=1, keepdims=True)
     weight = jnp.sum(inverse * half, axis=0, keepdims=True)
-    inner = weight + (infl_ref[0] * math.sqrt(MEMB - 1.0)) * inverse
+    inner = weight + (infl_ref[lax.axis_index("space") & 1] * math.sqrt(MEMB - 1.0)) * inverse
     out_ref[...] = 1.0 / MEMB + inner - jnp.sum(inner, axis=1, keepdims=True) * (1.0 / MEMB)
 
 
@@ -304,7 +311,7 @@
     )(ensemble)
     partial = pl.pallas_call(
         gram_kernel,
-        out_shape=pltpu.VMEM((SHARDS, 1, 2176), f32),
+        out_shape=pltpu.VMEM((SHARDS, 2, LINE * 128), f32),
         in_specs=[vmem, vmem, pl.BlockSpec(memory_space=pl.ANY)],
         out_specs=vmem,
         scratch_shapes=[
@@ -314,8 +321,8 @@
             pltpu.VMEM((512, 512), f32),
             pltpu.VMEM((2, NBLK, BLOCK), f32),
             pltpu.VMEM((2, NBLK, BLOCK), f32),
-            pltpu.VMEM((2 * MEMB + 16, 8 * BLOCK), bf16),
-            pltpu.VMEM((2 * MEMB + 16, 8 * BLOCK), bf16),
+            pltpu.VMEM((2 * MEMB + 16, CHUNKS * BLOCK), bf16),
+            pltpu.VMEM((2 * MEMB + 16, CHUNKS * BLOCK), bf16),
             pltpu.VMEM((2, 2 * MEMB, MEMB + 16), f32),
         ],
         compiler_params=pltpu.CompilerParams(vmem_limit_bytes=30 * 2**20),
@@ -330,20 +337,22 @@
         out_specs=vmem,
         compiler_params=pltpu.CompilerParams(vmem_limit_bytes=20 * 2**20),
         name="transform",
-    )(jnp.where(second, inflation[1:], inflation[:1]), parts)
+    )(inflation, parts)
     paired = lax.ppermute(made, "space", [(i, i ^ 1) for i in range(SHARDS)])
     early, late = jnp.where(second, paired, made), jnp.where(second, made, paired)
     product = times(late, early)
     place = lax.axis_index("tm")
+    y = place // 2
     eye = jnp.eye(MEMB, dtype=f32)
-    suffix = eye
-    for bit in (1, 2, 4):
-        other = lax.ppermute(product, "tm", [(i, i ^ bit) for i in range(8)])
-        first = (place & bit) == 0
-        ahead = jnp.where(first, other, eye)
-        suffix = ahead if bit == 1 else times(ahead, suffix)
-        if bit < 4:
-            product = times(jnp.where(first, other, product), jnp.where(first, product, other))
+    other = lax.ppermute(product, "tm", [(i, i ^ 1) for i in range(8)])
+    first = (place & 1) == 0
+    ahead = jnp.where(first, other, eye)
+    product = times(jnp.where(first, other, product), jnp.where(first, product, other))
+    one, two, three = (lax.ppermute(product, "tm", [(i, i ^ (2 * d)) for i in range(8)]) for d in (1, 2, 3))
+    nearest = jnp.where(y == 3, eye, jnp.where(y == 1, three, one))
+    middle = jnp.where(y < 2, two, eye)
+    farthest = jnp.where(y == 0, three, eye)
+    suffix = times(times(farthest, middle), times(nearest, ahead))
     return pl.pallas_call(
         apply_kernel,
         out_shape=jax.ShapeDtypeStruct((2, MEMB, CELLS), f32),

time: 73.4 us -> 72.4 us (0.986)
  blocking collectives: 0 us -> 16.2 us
  waiting for transfers between devices: 28.8 us -> 16.2 us
  starting transfers between devices: 20.3 us -> 17.5 us
  between operations: 1.37 us -> 0.09 us
    all_to_all x0 -> x1, blocking collectives: none -> 16.2 us  [body(): lax.all_to_all(partial, 'space', split_axis=0, concat_axis=0, tiled=True)]
    all_to_all x1 -> x0, waiting for transfers between devices: 10.1 us -> none  [body(): lax.all_to_all(partial, 'space', split_axis=0, concat_axis=0, tiled=True)]
    all_to_all x1 -> x0, starting transfers between devices: 4.15 us -> none  [body(): lax.all_to_all(partial, 'space', split_axis=0, concat_axis=0, tiled=True)]
    ppermute x3 -> x4, waiting for transfers between devices: 7.61 us -> 5.19 us  [the longest x3 4 us: body(): lax.ppermute(product, 'tm', [(i, i ^ 2 * d) for i in range(8)])]
    ppermute x3 -> x4, starting transfers between devices: 3 us -> 4.27 us  [the longest x3 4.18 us: body(): lax.ppermute(product, 'tm', [(i, i ^ 2 * d) for i in range(8)])]
    pallas_call x1, Pallas kernels: 8.77 us -> 7.59 us  [body(): pl.pallas_call(gram_kernel, out_shape=pltpu.VMEM((SHARDS, 2, LINE * 128),...]
  transfers between devices with their start and end apart: 6 -> 6, of which waited for: 6 -> 5; matrix products, arithmetic and copies ran while one was open for 1% -> 0% of each run, Pallas kernels for 3% -> 3%
where the time goes in v3:
time: 72.4 us; the launch traced here: 71.3 us
  Pallas kernels  20.5 us (28%)
  starting transfers between devices  17.5 us (24%)
  waiting for transfers between devices  16.2 us (22%)
  blocking collectives  16.2 us (22%)
  matrix products  0.81 us (1%)
    all_to_all x1, blocking collectives, body(): lax.all_to_all(partial, 'space', split_axis=0, concat_axis=0, tiled=True)  16.2 us
    all_to_all x1, starting transfers between devices, body(): lax.all_to_all(routed, 'space', split_axis=0, concat_axis=0, tiled=True)  11.3 us
    all_to_all x1, waiting for transfers between devices, body(): lax.all_to_all(routed, 'space', split_axis=0, concat_axis=0, tiled=True)  8.96 us
    pallas_call x1, Pallas kernels, body(): pl.pallas_call(gram_kernel, out_shape=pltpu.VMEM((SHARDS, 2, LINE * 128),...  7.59 us
    pallas_call x1, Pallas kernels, body(): pl.pallas_call(apply_kernel, out_shape=jax.ShapeDtypeStruct((2, MEMB, CEL...  4.89 us
    ppermute x3, starting transfers between devices, body(): lax.ppermute(product, 'tm', [(i, i ^ 2 * d) for i in range(8)])  4.18 us
    ppermute x3, waiting for transfers between devices, body(): lax.ppermute(product, 'tm', [(i, i ^ 2 * d) for i in range(8)])  4 us
    pallas_call x1, Pallas kernels, body(): pl.pallas_call(transform_kernel, out_shape=pltpu.VMEM((MEMB, MEMB), f32),...  3.64 us
  transfers between devices with their start and end apart: 6, of which 5 were waited for; matrix products, arithmetic and copies ran while one was open for 0% of the time, Pallas kernels for 3%

profile of v3, /device:TPU:8, one launch (start us, length us, event | category | flops | bytes accessed | tf_op | source)
XLA Modules:
  0.0 71.3 jit_solution(1813548507476825966)
XLA Ops:
  0.0 0.0 copy-start
  0.0 2.1 %route.1 = f32[32,3,4,128]{3,2,1,0:T(4,128)} custom-call(s32[2,128]{1,0:T(2,128)} %bitcast.11, s32[2,128]{1,0:T(2,128)} %local_ref.1, s32[2,32,128]{2,1,0:T(8,128)} %bitcast.8, s32[2,128]{1,0:T(2,128)} %count_ref.1, f32[2,32,128]{2,1,0:T(8,128)} %bitcast.9, f32[2,32,128]{2,1,0:T(8,128)} %bitcast.10), custom_call_target="tpu_custom_call" | custom-call | tf_op jit(solution)/shard_map/route/pallas_call | solution.py:294
  2.1 11.3 %all-to-all-start = ((f32[32,3,4,128]{3,2,1,0:T(4,128)}), f32[32,3,4,128]{3,2,1,0:T(4,128)S(1)}, u32[]{:S(2)}, u32[]{:S(2)}) async-start(f32[32,3,4,128]{3,2,1,0:T(4,128)} %route.1), calls=%async_computation | async-start | bytes 393216 | tf_op jit(solution)/shard_map/all_to_all | solution.py:301
  13.4 2.3 %center.1.mean_ref = f32[2,64,256]{2,1,0:T(8,128)S(1)} custom-call(bf16[2,64,16384]{2,1,0:T(8,128)(2,1)} %ens_hbm.5), custom_call_target="tpu_custom_call" | custom-call | tf_op jit(solution)/shard_map/center/pallas_call | solution.py:303
  15.7 9.0 %all-to-all-done.recv_ref = f32[32,3,4,128]{3,2,1,0:T(4,128)S(1)} async-done(((f32[32,3,4,128]{3,2,1,0:T(4,128)}), f32[32,3,4,128]{3,2,1,0:T(4,128)S(1)}, u32[]{:S(2)}, u32[]{:S(2)}) %all-to-all-start) | async-done | bytes 196640 | tf_op jit(solution)/shard_map/all_to_all | solution.py:301
  24.7 7.6 %gram.1 = f32[32,2,1152]{2,1,0:T(2,128)S(1)} custom-call(f32[32,3,4,128]{3,2,1,0:T(4,128)S(1)} %all-to-all-done.recv_ref, f32[2,64,256]{2,1,0:T(8,128)S(1)} %center.1.mean_ref, bf16[2,64,16384]{2,1,0:T(8,128)(2,1)} %ens_hbm.5), custom_call_target="tpu_custom_call" | custom-call | tf_op jit(solution)/shard_map/gram/pallas_call | solution.py:312
  32.3 16.2 %all_to_all.10.parts_ref = f32[32,2,1152]{2,1,0:T(2,128)S(1)} all-to-all(f32[32,2,1152]{2,1,0:T(2,128)S(1)} %gram.1), channel_id=1, replica_groups=mesh['tm'=8,'space'=32] {'space'}, dimensions={0} | all-to-all | bytes 589824 | tf_op jit(solution)/shard_map/all_to_all | solution.py:331
  48.5 0.0 copy-done
  48.5 3.6 %transform.1 = f32[64,64]{1,0:T(8,128)S(1)} custom-call(f32[2]{0:T(128)S(1)} %copy-done, f32[32,2,1152]{2,1,0:T(2,128)S(1)} %all_to_all.10.parts_ref), custom_call_target="tpu_custom_call" | custom-call | tf_op jit(solution)/shard_map/transform/pallas_call | solution.py:333
  52.2 1.9 %collective-permute-start = (f32[64,64]{1,0:T(8,128)S(1)}, f32[64,64]{1,0:T(8,128)S(1)}, u32[]{:S(2)}, u32[]{:S(2)}) collective-permute-start(f32[64,64]{1,0:T(8,128)S(1)} %transform.1), channel_id=1, source_target_pairs={{0,1},{1,0},{2,3},{3,2},{4,5},{5,4},{6,7},{7,6},{8,9},{9,8},{10,11... | collective-permute-start | bytes 49160 | tf_op jit(solution)/shard_map/ppermute | solution.py:341
  54.0 2.1 %collective-permute-done = f32[64,64]{1,0:T(8,128)S(1)} collective-permute-done((f32[64,64]{1,0:T(8,128)S(1)}, f32[64,64]{1,0:T(8,128)S(1)}, u32[]{:S(2)}, u32[]{:S(2)}) %collective-permute-start) | collective-permute-done | bytes 16416 | tf_op jit(solution)/shard_map/ppermute | solution.py:341
  56.1 0.2 fusion.12
  56.3 0.1 collective-permute-start.1
  56.4 1.2 %collective-permute-done.1 = f32[64,64]{1,0:T(8,128)S(1)} collective-permute-done((f32[64,64]{1,0:T(8,128)S(1)}, f32[64,64]{1,0:T(8,128)S(1)}, u32[]{:S(2)}, u32[]{:S(2)}) %collective-permute-start.1) | collective-permute-done | bytes 16416 | tf_op jit(solution)/shard_map/ppermute | solution.py:347
  57.6 0.2 fusion.3
  57.8 0.5 collective-permute-start.4
  58.3 2.4 %collective-permute-start.2 = (f32[64,64]{1,0:T(8,128)S(1)}, f32[64,64]{1,0:T(8,128)S(1)}, u32[]{:S(2)}, u32[]{:S(2)}) collective-permute-start(f32[64,64]{1,0:T(8,128)S(1)} %fusion.3), channel_id=1, source_target_pairs={{0,192},{32,224},{64,128},{96,160},{128,64},{160,96},{192,0},{224,... | collective-permute-start | bytes 49160 | tf_op jit(solution)/shard_map/ppermute | solution.py:351
  60.7 1.2 %collective-permute-start.3 = (f32[64,64]{1,0:T(8,128)S(1)}, f32[64,64]{1,0:T(8,128)S(1)}, u32[]{:S(2)}, u32[]{:S(2)}) collective-permute-start(f32[64,64]{1,0:T(8,128)S(1)} %fusion.3), channel_id=1, source_target_pairs={{0,128},{32,160},{64,192},{96,224},{128,0},{160,32},{192,64},{224,... | collective-permute-start | bytes 49160 | tf_op jit(solution)/shard_map/ppermute | solution.py:351
  61.9 0.0 collective-permute-done.4
  61.9 0.6 collective-permute-done.2
  62.6 0.2 fusion.1
  62.8 3.4 %collective-permute-done.3 = f32[64,64]{1,0:T(8,128)S(1)} collective-permute-done((f32[64,64]{1,0:T(8,128)S(1)}, f32[64,64]{1,0:T(8,128)S(1)}, u32[]{:S(2)}, u32[]{:S(2)}) %collective-permute-start.3) | collective-permute-done | bytes 16416 | tf_op jit(solution)/shard_map/ppermute | solution.py:351
  66.1 0.2 fusion
  66.3 0.2 fusion.13.suffix_ref
  66.5 4.9 %apply.1 = f32[2,64,16384]{2,1,0:T(8,128)} custom-call(f32[64,64]{1,0:T(8,128)S(1)} %fusion.13.suffix_ref, f32[64,64]{1,0:T(8,128)S(1)} %get-tuple-element.5.first_ref, f32[64,64]{1,0:T(8,128)S(1)} %get-tuple-element.6.second_ref, bf16[2,64,16384]{2,1,0:T(8,128)(2,1)} %ens_hbm.5), custom_call_target="tpu_custom_call" | custom-call | tf_op jit(solution)/shard_map/apply/pallas_call | solution.py:356
  (1 shorter events, 0.0 us)
Async XLA Ops:
  0.0 48.5 %copy-start = (f32[2]{0:T(128)S(1)}, f32[2]{0:T(128)}, u32[]{:S(2)}) copy-start(f32[2]{0:T(128)} %infl_ref.1) | copy-start | bytes 28
  2.1 22.6 %all-to-all-start = ((f32[32,3,4,128]{3,2,1,0:T(4,128)}), f32[32,3,4,128]{3,2,1,0:T(4,128)S(1)}, u32[]{:S(2)}, u32[]{:S(2)}) async-start(f32[32,3,4,128]{3,2,1,0:T(4,128)} %route.1), calls=%async_computation | async-start | bytes 393216 | tf_op jit(solution)/shard_map/all_to_all | solution.py:301
  52.2 4.0 %collective-permute-start = (f32[64,64]{1,0:T(8,128)S(1)}, f32[64,64]{1,0:T(8,128)S(1)}, u32[]{:S(2)}, u32[]{:S(2)}) collective-permute-start(f32[64,64]{1,0:T(8,128)S(1)} %transform.1), channel_id=1, source_target_pairs={{0,1},{1,0},{2,3},{3,2},{4,5},{5,4},{6,7},{7,6},{8,9},{9,8},{10,11... | collective-permute-start | bytes 49160 | tf_op jit(solution)/shard_map/ppermute | solution.py:341
  56.3 1.3 %collective-permute-start.1 = (f32[64,64]{1,0:T(8,128)S(1)}, f32[64,64]{1,0:T(8,128)S(1)}, u32[]{:S(2)}, u32[]{:S(2)}) collective-permute-start(f32[64,64]{1,0:T(8,128)S(1)} %fusion.12), channel_id=1, source_target_pairs={{0,32},{32,0},{64,96},{96,64},{128,160},{160,128},{192,224},{224,1... | collective-permute-start | bytes 49160 | tf_op jit(solution)/shard_map/ppermute | solution.py:347
  57.8 4.2 %collective-permute-start.4 = (f32[64,64]{1,0:T(8,128)S(1)}, f32[64,64]{1,0:T(8,128)S(1)}, u32[]{:S(2)}, u32[]{:S(2)}) collective-permute-start(f32[64,64]{1,0:T(8,128)S(1)} %fusion.3), channel_id=1, source_target_pairs={{0,64},{32,96},{64,0},{96,32},{128,192},{160,224},{192,128},{224,1... | collective-permute-start | bytes 49160 | tf_op jit(solution)/shard_map/ppermute | solution.py:351
  58.3 4.3 %collective-permute-start.2 = (f32[64,64]{1,0:T(8,128)S(1)}, f32[64,64]{1,0:T(8,128)S(1)}, u32[]{:S(2)}, u32[]{:S(2)}) collective-permute-start(f32[64,64]{1,0:T(8,128)S(1)} %fusion.3), channel_id=1, source_target_pairs={{0,192},{32,224},{64,128},{96,160},{128,64},{160,96},{192,0},{224,... | collective-permute-start | bytes 49160 | tf_op jit(solution)/shard_map/ppermute | solution.py:351
  60.7 5.4 %collective-permute-start.3 = (f32[64,64]{1,0:T(8,128)S(1)}, f32[64,64]{1,0:T(8,128)S(1)}, u32[]{:S(2)}, u32[]{:S(2)}) collective-permute-start(f32[64,64]{1,0:T(8,128)S(1)} %fusion.3), channel_id=1, source_target_pairs={{0,128},{32,160},{64,192},{96,224},{128,0},{160,32},{192,64},{224,... | collective-permute-start | bytes 49160 | tf_op jit(solution)/shard_map/ppermute | solution.py:351

commit v4 on v3

--- a/solution.py
+++ b/solution.py
@@ -18,7 +18,7 @@
 HALF = MEMB // 2
 LINE = 9
 STEP = 8
-WIDTH = 4096
+PIECES = ((1, 0, 2048), (1, 2048, 2048), (1, 4096, 4096), (1, 8192, 8192), (0, 0, 8192), (0, 8192, 8192))
 
 f32 = jnp.float32
 bf16 = jnp.bfloat16
@@ -196,9 +196,8 @@
     found = [[] for _ in systems]
     full = (8, 2 * MEMB)
     for j in range(0, MEMB, STEP):
-        t, s = divmod(j, 8)
         for w in range(count):
-            rows = [jnp.broadcast_to(tiles[w][t][s + k : s + k + 1, :], full) for k in range(STEP)]
+            rows = [jnp.broadcast_to(tiles[w][(j + k) // 8][(j + k) % 8][None], full) for k in range(STEP)]
             block = [
                 [jnp.broadcast_to(rows[k][:, j + l : j + l + 1], full) if l >= k else None for l in range(STEP)]
                 for k in range(STEP)
@@ -215,7 +214,7 @@
                     rows[l] = rows[l] - lower[l][k] * rows[k]
             for k in range(STEP):
                 found[w].append(rows[k][:1, :] * lax.rsqrt(block[k][k][:1, :]))
-            first = t if s + STEP < 8 else t + 1
+            first = (j + STEP) // 8
             if first == MEMB // 8:
                 continue
             solved = [None] * STEP
@@ -253,7 +252,9 @@
     inverse = eliminate([gram + ridge])[0]
     half = jnp.sum(inverse * proj, axis=1, keepdims=True)
     weight = jnp.sum(inverse * half, axis=0, keepdims=True)
-    inner = weight + (infl_ref[lax.axis_index("space") & 1] * math.sqrt(MEMB - 1.0)) * inverse
+    odd = (lax.axis_index("space") & 1) == 1
+    inflation = jnp.where(odd, infl_ref[:, 1:2], infl_ref[:, 0:1])
+    inner = weight + (inflation * math.sqrt(MEMB - 1.0)) * inverse
     out_ref[...] = 1.0 / MEMB + inner - jnp.sum(inner, axis=1, keepdims=True) * (1.0 / MEMB)
 
 
@@ -261,24 +262,45 @@
     return jnp.dot(a, b, precision=exact_mode, preferred_element_type=f32)
 
 
-def apply_kernel(suffix_ref, first_ref, second_ref, ens_hbm, out_hbm, ens, out, in_sems, out_sems):
-    pieces = 16384 // WIDTH
-
-    def part(i):
-        return (i // pieces, slice(None), pl.ds(i % pieces * WIDTH, WIDTH))
-
-    reads = [pltpu.make_async_copy(ens_hbm.at[part(i)], ens.at[i], in_sems.at[i]) for i in range(2 * pieces)]
-    for copy in reads:
+def fetch_kernel(after_ref, ens_hbm, out_ref, sems):
+    copies = [pltpu.make_async_copy(ens_hbm.at[w], out_ref.at[w], sems.at[w]) for w in range(2)]
+    for copy in copies:
         copy.start()
-    last = exact(suffix_ref[...], second_ref[...])
-    totals = [exact(last, first_ref[...]), last]
+    for copy in copies:
+        copy.wait()
+
+
+def pair_kernel(made_ref, paired_ref, late_ref, product_ref):
+    odd = (lax.axis_index("space") & 1) == 1
+    late = jnp.where(odd, made_ref[...], paired_ref[...])
+    late_ref[...] = late
+    product_ref[...] = exact(late, jnp.where(odd, paired_ref[...], made_ref[...]))
+
+
+def join_kernel(product_ref, other_ref, ahead_ref, joined_ref):
+    earlier = (lax.axis_index("tm") & 1) == 0
+    product, other = product_ref[...], other_ref[...]
+    joined_ref[...] = exact(jnp.where(earlier, other, product), jnp.where(earlier, product, other))
+    eye = jnp.where(iota((MEMB, MEMB), 0) == iota((MEMB, MEMB), 1), 1.0, 0.0)
+    ahead_ref[...] = jnp.where(earlier, other, eye)
+
+
+def apply_kernel(one_ref, two_ref, three_ref, first_ref, second_ref, ens_ref, out_hbm, out, sems):
+    y = lax.axis_index("tm") // 2
+    eye = jnp.where(iota((MEMB, MEMB), 0) == iota((MEMB, MEMB), 1), 1.0, 0.0)
+    one, two, three = one_ref[...], two_ref[...], three_ref[...]
+    nearest = jnp.where(y == 3, eye, jnp.where(y == 1, three, one))
+    behind = exact(jnp.where(y == 0, three, eye), jnp.where(y < 2, two, eye))
+    totals = [exact(behind, exact(nearest, ref[...])) for ref in (first_ref, second_ref)]
     writes = []
-    for i in range(2 * pieces):
-        reads[i].wait()
-        both = jnp.concatenate(split(totals[i // pieces]), axis=1)
-        cells = ens[i]
-        out[i] = jnp.dot(both, jnp.concatenate([cells, cells], axis=0), preferred_element_type=f32)
-        writes.append(pltpu.make_async_copy(out.at[i], out_hbm.at[part(i)], out_sems.at[i]))
+    for i, (w, start, width) in enumerate(PIECES):
+        both = jnp.concatenate(split(totals[w]), axis=1)
+        here = slice(start, start + width)
+        cells = ens_ref[w, :, here]
+        out[w, :, here] = jnp.dot(both, jnp.concatenate([cells, cells], axis=0), preferred_element_type=f32)
+        writes.append(
+            pltpu.make_async_copy(out.at[w, :, pl.ds(start, width)], out_hbm.at[w, :, pl.ds(start, width)], sems.at[i])
+        )
         writes[i].start()
     for copy in writes:
         copy.wait()
@@ -329,44 +351,56 @@
         name="gram",
     )(recv, means, ensemble)
     parts = lax.all_to_all(partial, "space", split_axis=0, concat_axis=0, tiled=True)
-    second = (lax.axis_index("space") & 1) == 1
     made = pl.pallas_call(
         transform_kernel,
         out_shape=pltpu.VMEM((MEMB, MEMB), f32),
-        in_specs=[pl.BlockSpec(memory_space=pltpu.SMEM), vmem],
+        in_specs=[vmem, vmem],
         out_specs=vmem,
         compiler_params=pltpu.CompilerParams(vmem_limit_bytes=20 * 2**20),
         name="transform",
-    )(inflation, parts)
+    )(inflation[None], parts)
     paired = lax.ppermute(made, "space", [(i, i ^ 1) for i in range(SHARDS)])
-    early, late = jnp.where(second, paired, made), jnp.where(second, made, paired)
-    product = times(late, early)
-    place = lax.axis_index("tm")
-    y = place // 2
-    eye = jnp.eye(MEMB, dtype=f32)
+    held = pl.pallas_call(
+        fetch_kernel,
+        out_shape=pltpu.VMEM((2, MEMB, CELLS), bf16),
+        in_specs=[pl.BlockSpec(memory_space=pl.ANY)] * 2,
+        out_specs=vmem,
+        scratch_shapes=[pltpu.SemaphoreType.DMA((2,))],
+        compiler_params=pltpu.CompilerParams(vmem_limit_bytes=4 * 2**20),
+        name="fetch",
+    )(made, ensemble)
+    square = pltpu.VMEM((MEMB, MEMB), f32)
+    small = pltpu.CompilerParams(vmem_limit_bytes=4 * 2**20)
+    late, product = pl.pallas_call(
+        pair_kernel,
+        out_shape=(square, square),
+        in_specs=[vmem] * 2,
+        out_specs=(vmem, vmem),
+        compiler_params=small,
+        name="pair",
+    )(made, paired)
     other = lax.ppermute(product, "tm", [(i, i ^ 1) for i in range(8)])
-    first = (place & 1) == 0
-    ahead = jnp.where(first, other, eye)
-    product = times(jnp.where(first, other, product), jnp.where(first, product, other))
-    one, two, three = (lax.ppermute(product, "tm", [(i, i ^ (2 * d)) for i in range(8)]) for d in (1, 2, 3))
-    nearest = jnp.where(y == 3, eye, jnp.where(y == 1, three, one))
-    middle = jnp.where(y < 2, two, eye)
-    farthest = jnp.where(y == 0, three, eye)
-    suffix = times(times(farthest, middle), times(nearest, ahead))
+    ahead, joined = pl.pallas_call(
+        join_kernel,
+        out_shape=(square, square),
+        in_specs=[vmem] * 2,
+        out_specs=(vmem, vmem),
+        compiler_params=small,
+        name="join",
+    )(product, other)
+    turned_by = {}
+    for name, bits in (("far", 6), ("middle", 4), ("near", 2)):
+        turned_by[name] = lax.ppermute(joined, "tm", [(i, i ^ bits) for i in range(8)])
+    one, two, three = turned_by["near"], turned_by["middle"], turned_by["far"]
     return pl.pallas_call(
         apply_kernel,
         out_shape=jax.ShapeDtypeStruct((2, MEMB, CELLS), f32),
-        in_specs=[vmem, vmem, vmem, pl.BlockSpec(memory_space=pl.ANY)],
+        in_specs=[vmem] * 6,
         out_specs=pl.BlockSpec(memory_space=pl.ANY),
-        scratch_shapes=[
-            pltpu.VMEM((2 * CELLS // WIDTH, MEMB, WIDTH), bf16),
-            pltpu.VMEM((2 * CELLS // WIDTH, MEMB, WIDTH), f32),
-            pltpu.SemaphoreType.DMA((2 * CELLS // WIDTH,)),
-            pltpu.SemaphoreType.DMA((2 * CELLS // WIDTH,)),
-        ],
+        scratch_shapes=[pltpu.VMEM((2, MEMB, CELLS), f32), pltpu.SemaphoreType.DMA((len(PIECES),))],
         compiler_params=pltpu.CompilerParams(vmem_limit_bytes=30 * 2**20),
         name="apply",
-    )(suffix, early, late, ensemble)
+    )(one, two, three, times(ahead, product), times(ahead, late), held)
 
 
 def solution(mesh):

time: 72.4 us -> 71.2 us (0.983)
  the two profiles are of different devices: /device:TPU:8 before, /device:TPU:1 now
where the time goes in v4:
time: 71.2 us; the launch traced here: 71 us
  starting transfers between devices  22.2 us (31%)
  Pallas kernels  21.8 us (31%)
  blocking collectives  15 us (21%)
  waiting for transfers between devices  11.6 us (16%)
    all_to_all x1, blocking collectives, body(): lax.all_to_all(partial, 'space', split_axis=0, concat_axis=0, tiled=True)  15 us
    all_to_all x1, starting transfers between devices, body(): lax.all_to_all(routed, 'space', split_axis=0, concat_axis=0, tiled=True)  11.9 us
    pallas_call x1, Pallas kernels, body(): pl.pallas_call(gram_kernel, out_shape=pltpu.VMEM((SHARDS, 2, LINE * 128),...  7.6 us
    all_to_all x1, waiting for transfers between devices, body(): lax.all_to_all(routed, 'space', split_axis=0, concat_axis=0, tiled=True)  7.03 us
    pallas_call x1, Pallas kernels, body(): pl.pallas_call(apply_kernel, out_shape=jax.ShapeDtypeStruct((2, MEMB, CEL...  4.11 us
    ppermute x1, starting transfers between devices, body(): other = lax.ppermute(product, 'tm', [(i, i ^ 1) for i in range(8)])  3.61 us
    ppermute x3, starting transfers between devices, body(): lax.ppermute(joined, 'tm', [(i, i ^ bits) for i in range(8)])  3.5 us
    ppermute x3, waiting for transfers between devices, body(): lax.ppermute(joined, 'tm', [(i, i ^ bits) for i in range(8)])  3.26 us
  transfers between devices with their start and end apart: 6, of which 4 were waited for; matrix products, arithmetic and copies ran while one was open for 0% of the time, Pallas kernels for 6%

profile of v4, /device:TPU:1, one launch (start us, length us, event | category | flops | bytes accessed | tf_op | source)
XLA Modules:
  0.0 71.0 jit_solution(9943718030924909530)
XLA Ops:
  0.0 2.0 %route.1 = f32[32,3,4,128]{3,2,1,0:T(4,128)} custom-call(s32[2,128]{1,0:T(2,128)} %bitcast.13, s32[2,128]{1,0:T(2,128)} %local_ref.1, s32[2,32,128]{2,1,0:T(8,128)} %bitcast.10, s32[2,128]{1,0:T(2,128)} %count_ref.1, f32[2,32,128]{2,1,0:T(8,128)} %bitcast.11, f32[2,32,128]{2,1,0:T(8,128)} %bitcast.12), custom_call_target="tpu_custom_call" | custom-call | tf_op jit(solution)/shard_map/route/pallas_call | solution.py:316
  2.0 11.9 %all-to-all-start = ((f32[32,3,4,128]{3,2,1,0:T(4,128)}), f32[32,3,4,128]{3,2,1,0:T(4,128)S(1)}, u32[]{:S(2)}, u32[]{:S(2)}) async-start(f32[32,3,4,128]{3,2,1,0:T(4,128)} %route.1), calls=%async_computation | async-start | bytes 393216 | tf_op jit(solution)/shard_map/all_to_all | solution.py:323
  13.9 0.0 copy-start
  13.9 2.3 %center.1.mean_ref = f32[2,64,256]{2,1,0:T(8,128)S(1)} custom-call(bf16[2,64,16384]{2,1,0:T(8,128)(2,1)} %ens_hbm.5), custom_call_target="tpu_custom_call" | custom-call | tf_op jit(solution)/shard_map/center/pallas_call | solution.py:325
  16.3 7.0 %all-to-all-done.recv_ref = f32[32,3,4,128]{3,2,1,0:T(4,128)S(1)} async-done(((f32[32,3,4,128]{3,2,1,0:T(4,128)}), f32[32,3,4,128]{3,2,1,0:T(4,128)S(1)}, u32[]{:S(2)}, u32[]{:S(2)}) %all-to-all-start) | async-done | bytes 196640 | tf_op jit(solution)/shard_map/all_to_all | solution.py:323
  23.3 7.6 %gram.1 = f32[32,2,1152]{2,1,0:T(2,128)S(1)} custom-call(f32[32,3,4,128]{3,2,1,0:T(4,128)S(1)} %all-to-all-done.recv_ref, f32[2,64,256]{2,1,0:T(8,128)S(1)} %center.1.mean_ref, bf16[2,64,16384]{2,1,0:T(8,128)(2,1)} %ens_hbm.5), custom_call_target="tpu_custom_call" | custom-call | tf_op jit(solution)/shard_map/gram/pallas_call | solution.py:334
  30.9 15.0 %all_to_all.10.parts_ref = f32[32,2,1152]{2,1,0:T(2,128)S(1)} all-to-all(f32[32,2,1152]{2,1,0:T(2,128)S(1)} %gram.1), channel_id=1, replica_groups=mesh['tm'=8,'space'=32] {'space'}, dimensions={0} | all-to-all | bytes 589824 | tf_op jit(solution)/shard_map/all_to_all | solution.py:353
  45.9 0.0 copy-done
  45.9 3.1 %transform.1.made_ref.after_ref = f32[64,64]{1,0:T(8,128)S(1)} custom-call(f32[1,2]{1,0:T(1,128)S(1)} %bitcast.9, f32[32,2,1152]{2,1,0:T(2,128)S(1)} %all_to_all.10.parts_ref), custom_call_target="tpu_custom_call" | custom-call | tf_op jit(solution)/shard_map/transform/pallas_call | solution.py:354
  49.1 3.2 %collective-permute-start = (f32[64,64]{1,0:T(8,128)S(1)}, f32[64,64]{1,0:T(8,128)S(1)}, u32[]{:S(2)}, u32[]{:S(2)}) collective-permute-start(f32[64,64]{1,0:T(8,128)S(1)} %transform.1.made_ref.after_ref), channel_id=1, source_target_pairs={{0,1},{1,0},{2,3},{3,2},{4,5},{5,4},{6,7},{7,6},{8,9},{9,8},{10,11... | collective-permute-start | bytes 49160 | tf_op jit(solution)/shard_map/ppermute | solution.py:362
  52.2 1.3 %collective-permute-done.paired_ref = f32[64,64]{1,0:T(8,128)S(1)} collective-permute-done((f32[64,64]{1,0:T(8,128)S(1)}, f32[64,64]{1,0:T(8,128)S(1)}, u32[]{:S(2)}, u32[]{:S(2)}) %collective-permute-start) | collective-permute-done | bytes 16416 | tf_op jit(solution)/shard_map/ppermute | solution.py:362
  53.5 0.2 pair.1
  53.7 3.6 %collective-permute-start.1 = (f32[64,64]{1,0:T(8,128)S(1)}, f32[64,64]{1,0:T(8,128)S(1)}, u32[]{:S(2)}, u32[]{:S(2)}) collective-permute-start(f32[64,64]{1,0:T(8,128)S(1)} %get-tuple-element.9.product_ref), channel_id=1, source_target_pairs={{0,32},{32,0},{64,96},{96,64},{128,160},{160,128},{192,224},{224,1... | collective-permute-start | bytes 49160 | tf_op jit(solution)/shard_map/ppermute | solution.py:382
  57.3 2.2 %fetch.1.ens_ref = bf16[2,64,16384]{2,1,0:T(8,128)(2,1)S(1)} custom-call(f32[64,64]{1,0:T(8,128)S(1)} %transform.1.made_ref.after_ref, bf16[2,64,16384]{2,1,0:T(8,128)(2,1)} %ens_hbm.5), custom_call_target="tpu_custom_call" | custom-call | tf_op jit(solution)/shard_map/fetch/pallas_call | solution.py:363
  59.6 0.0 collective-permute-done.1.other_ref
  59.6 0.2 join.1
  59.8 2.8 %collective-permute-start.4 = (f32[64,64]{1,0:T(8,128)S(1)}, f32[64,64]{1,0:T(8,128)S(1)}, u32[]{:S(2)}, u32[]{:S(2)}) collective-permute-start(f32[64,64]{1,0:T(8,128)S(1)} %get-tuple-element.10), channel_id=1, source_target_pairs={{0,192},{32,224},{64,128},{96,160},{128,64},{160,96},{192,0},{224,... | collective-permute-start | bytes 49160 | tf_op jit(solution)/shard_map/ppermute | solution.py:393
  62.6 0.3 collective-permute-start.3
  62.9 0.3 collective-permute-start.2
  63.3 0.2 fusion.first_ref
  63.4 0.2 fusion.1.second_ref
  63.6 0.3 collective-permute-done.4.three_ref
  63.9 3.0 %collective-permute-done.3.two_ref = f32[64,64]{1,0:T(8,128)S(1)} collective-permute-done((f32[64,64]{1,0:T(8,128)S(1)}, f32[64,64]{1,0:T(8,128)S(1)}, u32[]{:S(2)}, u32[]{:S(2)}) %collective-permute-start.3) | collective-permute-done | bytes 16416 | tf_op jit(solution)/shard_map/ppermute | solution.py:393
  66.9 0.0 collective-permute-done.2.one_ref
  66.9 4.1 %apply.1 = f32[2,64,16384]{2,1,0:T(8,128)} custom-call(f32[64,64]{1,0:T(8,128)S(1)} %collective-permute-done.2.one_ref, f32[64,64]{1,0:T(8,128)S(1)} %collective-permute-done.3.two_ref, f32[64,64]{1,0:T(8,128)S(1)} %collective-permute-done.4.three_ref, f32[64,64]{1,0:T(8,128)S(1)} %fusion.first_ref, f32[64,64]{1,0:T(8,128)S(1)} %fusion.1.second_ref, ...), custom_call_target="tpu_custom_call" | custom-call | tf_op jit(solution)/shard_map/apply/pallas_call | solution.py:395
Async XLA Ops:
  2.0 21.3 %all-to-all-start = ((f32[32,3,4,128]{3,2,1,0:T(4,128)}), f32[32,3,4,128]{3,2,1,0:T(4,128)S(1)}, u32[]{:S(2)}, u32[]{:S(2)}) async-start(f32[32,3,4,128]{3,2,1,0:T(4,128)} %route.1), calls=%async_computation | async-start | bytes 393216 | tf_op jit(solution)/shard_map/all_to_all | solution.py:323
  13.9 32.0 %copy-start = (f32[2]{0:T(128)S(1)}, f32[2]{0:T(128)}, u32[]{:S(2)}) copy-start(f32[2]{0:T(128)} %param.15) | copy-start | bytes 28
  49.1 4.5 %collective-permute-start = (f32[64,64]{1,0:T(8,128)S(1)}, f32[64,64]{1,0:T(8,128)S(1)}, u32[]{:S(2)}, u32[]{:S(2)}) collective-permute-start(f32[64,64]{1,0:T(8,128)S(1)} %transform.1.made_ref.after_ref), channel_id=1, source_target_pairs={{0,1},{1,0},{2,3},{3,2},{4,5},{5,4},{6,7},{7,6},{8,9},{9,8},{10,11... | collective-permute-start | bytes 49160 | tf_op jit(solution)/shard_map/ppermute | solution.py:362
  53.7 5.9 %collective-permute-start.1 = (f32[64,64]{1,0:T(8,128)S(1)}, f32[64,64]{1,0:T(8,128)S(1)}, u32[]{:S(2)}, u32[]{:S(2)}) collective-permute-start(f32[64,64]{1,0:T(8,128)S(1)} %get-tuple-element.9.product_ref), channel_id=1, source_target_pairs={{0,32},{32,0},{64,96},{96,64},{128,160},{160,128},{192,224},{224,1... | collective-permute-start | bytes 49160 | tf_op jit(solution)/shard_map/ppermute | solution.py:382
  59.8 4.1 %collective-permute-start.4 = (f32[64,64]{1,0:T(8,128)S(1)}, f32[64,64]{1,0:T(8,128)S(1)}, u32[]{:S(2)}, u32[]{:S(2)}) collective-permute-start(f32[64,64]{1,0:T(8,128)S(1)} %get-tuple-element.10), channel_id=1, source_target_pairs={{0,192},{32,224},{64,128},{96,160},{128,64},{160,96},{192,0},{224,... | collective-permute-start | bytes 49160 | tf_op jit(solution)/shard_map/ppermute | solution.py:393
  62.6 4.3 %collective-permute-start.3 = (f32[64,64]{1,0:T(8,128)S(1)}, f32[64,64]{1,0:T(8,128)S(1)}, u32[]{:S(2)}, u32[]{:S(2)}) collective-permute-start(f32[64,64]{1,0:T(8,128)S(1)} %get-tuple-element.10), channel_id=1, source_target_pairs={{0,128},{32,160},{64,192},{96,224},{128,0},{160,32},{192,64},{224,... | collective-permute-start | bytes 49160 | tf_op jit(solution)/shard_map/ppermute | solution.py:393
  62.9 3.9 %collective-permute-start.2 = (f32[64,64]{1,0:T(8,128)S(1)}, f32[64,64]{1,0:T(8,128)S(1)}, u32[]{:S(2)}, u32[]{:S(2)}) collective-permute-start(f32[64,64]{1,0:T(8,128)S(1)} %get-tuple-element.10), channel_id=1, source_target_pairs={{0,64},{32,96},{64,0},{96,32},{128,192},{160,224},{192,128},{224,1... | collective-permute-start | bytes 49160 | tf_op jit(solution)/shard_map/ppermute | solution.py:393

commit v5 on v4

--- a/solution.py
+++ b/solution.py
@@ -14,6 +14,7 @@
 NBLK = 64
 CELLS = NBLK * BLOCK
 CHUNKS = 16
+TILE = 32
 PER = NBLK // CHUNKS
 HALF = MEMB // 2
 LINE = 9
@@ -45,10 +46,16 @@
         placer = jnp.where(iota((2 * SHARDS, 128), 0) == target, 1.0, 0.0).astype(bf16)
         live = iota((SLOTS, 128), 0) < count_ref[w : w + 1, :]
         precision = jnp.where(live, 1.0 / var_ref[w], 0.0)
-        rows = jnp.concatenate(
-            [precision, precision * value_ref[w], (local_ref[w : w + 1, :] * BLOCK + offset_ref[w]).astype(f32)],
-            axis=0,
-        )
+        offsets = offset_ref[w].astype(f32)
+        weighted = precision * value_ref[w]
+        totals = [jnp.zeros((SLOTS, 128), f32)] * 2
+        for r in range(SLOTS):
+            equal = offsets == offsets[r : r + 1, :]
+            totals = [
+                total + jnp.where(equal, part[r : r + 1, :], 0.0) for total, part in zip(totals, (precision, weighted))
+            ]
+        cells = (local_ref[w : w + 1, :] * BLOCK).astype(f32) + offsets
+        rows = jnp.concatenate(totals + [cells], axis=0)
         wide = jnp.concatenate(
             [
                 jnp.where(rank % 4 == c, rows[SLOTS * q : SLOTS * q + SLOTS], 0.0)
@@ -106,20 +113,20 @@
         table[2, SLOTS * c : SLOTS * c + SLOTS, :] = table[2, SLOTS * c : SLOTS * c + SLOTS, :] - held * BLOCK
 
     def scatter(tile, carry):
-        base = pl.multiple_of(tile * 32, 32)
-        cells = (iota((32, 128), 0) + base).astype(f32)
+        base = pl.multiple_of(tile * TILE, TILE)
+        cells = (iota((TILE, 128), 0) + base).astype(f32)
         for c in range(4):
-            acc_u = jnp.zeros((32, 128), f32)
-            acc_t = jnp.zeros((32, 128), f32)
+            found_u = jnp.zeros((TILE, 128), f32)
+            found_t = jnp.zeros((TILE, 128), f32)
             for r in range(SLOTS * c, SLOTS * c + SLOTS):
                 hit = table[2, r : r + 1, :] == cells
-                acc_u += jnp.where(hit, table[0, r : r + 1, :], 0.0)
-                acc_t += jnp.where(hit, table[1, r : r + 1, :], 0.0)
-            dense[pl.ds(base, 32), 128 * c : 128 * c + 128] = acc_u
-            dense[pl.ds(base + 256, 32), 128 * c : 128 * c + 128] = acc_t
+                found_u = jnp.where(hit, table[0, r : r + 1, :], found_u)
+                found_t = jnp.where(hit, table[1, r : r + 1, :], found_t)
+            dense[pl.ds(base, TILE), 128 * c : 128 * c + 128] = found_u
+            dense[pl.ds(base + 256, TILE), 128 * c : 128 * c + 128] = found_t
         return carry
 
-    lax.fori_loop(0, 8, scatter, 0)
+    lax.fori_loop(0, BLOCK // TILE, scatter, 0)
     row, lane = iota((2 * NBLK, 128), 0), iota((2 * NBLK, 128), 1)
     ours = (row // NBLK) == (lane // NBLK)
     holder = jnp.concatenate(

time: 71.2 us -> 70.3 us (0.987)
  Pallas kernels: 21.8 us -> 20.8 us
    pallas_call x1, Pallas kernels: 7.6 us -> 6.63 us  [body(): pl.pallas_call(gram_kernel, out_shape=pltpu.VMEM((SHARDS, 2, LINE * 128),...]
  transfers between devices with their start and end apart: 6 -> 6, of which waited for: 4 -> 4; matrix products, arithmetic and copies ran while one was open for 0% -> 0% of each run, Pallas kernels for 6% -> 7%
where the time goes in v5:
time: 70.3 us; the launch traced here: 70 us
  starting transfers between devices  22.1 us (31%)
  Pallas kernels  20.8 us (30%)
  blocking collectives  15 us (21%)
  waiting for transfers between devices  11.6 us (17%)
    all_to_all x1, blocking collectives, body(): lax.all_to_all(partial, 'space', split_axis=0, concat_axis=0, tiled=True)  15 us
    all_to_all x1, starting transfers between devices, body(): lax.all_to_all(routed, 'space', split_axis=0, concat_axis=0, tiled=True)  11.9 us
    all_to_all x1, waiting for transfers between devices, body(): lax.all_to_all(routed, 'space', split_axis=0, concat_axis=0, tiled=True)  7.03 us
    pallas_call x1, Pallas kernels, body(): pl.pallas_call(gram_kernel, out_shape=pltpu.VMEM((SHARDS, 2, LINE * 128),...  6.63 us
    pallas_call x1, Pallas kernels, body(): pl.pallas_call(apply_kernel, out_shape=jax.ShapeDtypeStruct((2, MEMB, CEL...  4.11 us
    ppermute x1, starting transfers between devices, body(): other = lax.ppermute(product, 'tm', [(i, i ^ 1) for i in range(8)])  3.6 us
    ppermute x3, starting transfers between devices, body(): lax.ppermute(joined, 'tm', [(i, i ^ bits) for i in range(8)])  3.49 us
    ppermute x3, waiting for transfers between devices, body(): lax.ppermute(joined, 'tm', [(i, i ^ bits) for i in range(8)])  3.26 us
  transfers between devices with their start and end apart: 6, of which 4 were waited for; matrix products, arithmetic and copies ran while one was open for 0% of the time, Pallas kernels for 7%

profile of v5, /device:TPU:1, one launch (start us, length us, event | category | flops | bytes accessed | tf_op | source)
XLA Modules:
  0.0 70.0 jit_solution(6585200248654257574)
XLA Ops:
  0.0 2.1 %route.1 = f32[32,3,4,128]{3,2,1,0:T(4,128)} custom-call(s32[2,128]{1,0:T(2,128)} %bitcast.13, s32[2,128]{1,0:T(2,128)} %local_ref.1, s32[2,32,128]{2,1,0:T(8,128)} %bitcast.10, s32[2,128]{1,0:T(2,128)} %count_ref.1, f32[2,32,128]{2,1,0:T(8,128)} %bitcast.11, f32[2,32,128]{2,1,0:T(8,128)} %bitcast.12), custom_call_target="tpu_custom_call" | custom-call | tf_op jit(solution)/shard_map/route/pallas_call | solution.py:323
  2.1 11.9 %all-to-all-start = ((f32[32,3,4,128]{3,2,1,0:T(4,128)}), f32[32,3,4,128]{3,2,1,0:T(4,128)S(1)}, u32[]{:S(2)}, u32[]{:S(2)}) async-start(f32[32,3,4,128]{3,2,1,0:T(4,128)} %route.1), calls=%async_computation | async-start | bytes 393216 | tf_op jit(solution)/shard_map/all_to_all | solution.py:330
  13.9 0.0 copy-start
  13.9 2.3 %center.1.mean_ref = f32[2,64,256]{2,1,0:T(8,128)S(1)} custom-call(bf16[2,64,16384]{2,1,0:T(8,128)(2,1)} %ens_hbm.5), custom_call_target="tpu_custom_call" | custom-call | tf_op jit(solution)/shard_map/center/pallas_call | solution.py:332
  16.3 7.0 %all-to-all-done.recv_ref = f32[32,3,4,128]{3,2,1,0:T(4,128)S(1)} async-done(((f32[32,3,4,128]{3,2,1,0:T(4,128)}), f32[32,3,4,128]{3,2,1,0:T(4,128)S(1)}, u32[]{:S(2)}, u32[]{:S(2)}) %all-to-all-start) | async-done | bytes 196640 | tf_op jit(solution)/shard_map/all_to_all | solution.py:330
  23.3 6.6 %gram.1 = f32[32,2,1152]{2,1,0:T(2,128)S(1)} custom-call(f32[32,3,4,128]{3,2,1,0:T(4,128)S(1)} %all-to-all-done.recv_ref, f32[2,64,256]{2,1,0:T(8,128)S(1)} %center.1.mean_ref, bf16[2,64,16384]{2,1,0:T(8,128)(2,1)} %ens_hbm.5), custom_call_target="tpu_custom_call" | custom-call | tf_op jit(solution)/shard_map/gram/pallas_call | solution.py:341
  30.0 15.0 %all_to_all.10.parts_ref = f32[32,2,1152]{2,1,0:T(2,128)S(1)} all-to-all(f32[32,2,1152]{2,1,0:T(2,128)S(1)} %gram.1), channel_id=1, replica_groups=mesh['tm'=8,'space'=32] {'space'}, dimensions={0} | all-to-all | bytes 589824 | tf_op jit(solution)/shard_map/all_to_all | solution.py:360
  45.0 0.0 copy-done
  45.0 3.1 %transform.1.made_ref.after_ref = f32[64,64]{1,0:T(8,128)S(1)} custom-call(f32[1,2]{1,0:T(1,128)S(1)} %bitcast.9, f32[32,2,1152]{2,1,0:T(2,128)S(1)} %all_to_all.10.parts_ref), custom_call_target="tpu_custom_call" | custom-call | tf_op jit(solution)/shard_map/transform/pallas_call | solution.py:361
  48.1 3.2 %collective-permute-start = (f32[64,64]{1,0:T(8,128)S(1)}, f32[64,64]{1,0:T(8,128)S(1)}, u32[]{:S(2)}, u32[]{:S(2)}) collective-permute-start(f32[64,64]{1,0:T(8,128)S(1)} %transform.1.made_ref.after_ref), channel_id=1, source_target_pairs={{0,1},{1,0},{2,3},{3,2},{4,5},{5,4},{6,7},{7,6},{8,9},{9,8},{10,11... | collective-permute-start | bytes 49160 | tf_op jit(solution)/shard_map/ppermute | solution.py:369
  51.3 1.3 %collective-permute-done.paired_ref = f32[64,64]{1,0:T(8,128)S(1)} collective-permute-done((f32[64,64]{1,0:T(8,128)S(1)}, f32[64,64]{1,0:T(8,128)S(1)}, u32[]{:S(2)}, u32[]{:S(2)}) %collective-permute-start) | collective-permute-done | bytes 16416 | tf_op jit(solution)/shard_map/ppermute | solution.py:369
  52.6 0.2 pair.1
  52.8 3.6 %collective-permute-start.1 = (f32[64,64]{1,0:T(8,128)S(1)}, f32[64,64]{1,0:T(8,128)S(1)}, u32[]{:S(2)}, u32[]{:S(2)}) collective-permute-start(f32[64,64]{1,0:T(8,128)S(1)} %get-tuple-element.9.product_ref), channel_id=1, source_target_pairs={{0,32},{32,0},{64,96},{96,64},{128,160},{160,128},{192,224},{224,1... | collective-permute-start | bytes 49160 | tf_op jit(solution)/shard_map/ppermute | solution.py:389
  56.4 2.2 %fetch.1.ens_ref = bf16[2,64,16384]{2,1,0:T(8,128)(2,1)S(1)} custom-call(f32[64,64]{1,0:T(8,128)S(1)} %transform.1.made_ref.after_ref, bf16[2,64,16384]{2,1,0:T(8,128)(2,1)} %ens_hbm.5), custom_call_target="tpu_custom_call" | custom-call | tf_op jit(solution)/shard_map/fetch/pallas_call | solution.py:370
  58.6 0.0 collective-permute-done.1.other_ref
  58.6 0.2 join.1
  58.8 2.8 %collective-permute-start.4 = (f32[64,64]{1,0:T(8,128)S(1)}, f32[64,64]{1,0:T(8,128)S(1)}, u32[]{:S(2)}, u32[]{:S(2)}) collective-permute-start(f32[64,64]{1,0:T(8,128)S(1)} %get-tuple-element.10), channel_id=1, source_target_pairs={{0,192},{32,224},{64,128},{96,160},{128,64},{160,96},{192,0},{224,... | collective-permute-start | bytes 49160 | tf_op jit(solution)/shard_map/ppermute | solution.py:400
  61.6 0.4 collective-permute-start.3
  62.0 0.3 collective-permute-start.2
  62.3 0.2 fusion.first_ref
  62.5 0.2 fusion.1.second_ref
  62.6 0.3 collective-permute-done.4.three_ref
  62.9 3.0 %collective-permute-done.3.two_ref = f32[64,64]{1,0:T(8,128)S(1)} collective-permute-done((f32[64,64]{1,0:T(8,128)S(1)}, f32[64,64]{1,0:T(8,128)S(1)}, u32[]{:S(2)}, u32[]{:S(2)}) %collective-permute-start.3) | collective-permute-done | bytes 16416 | tf_op jit(solution)/shard_map/ppermute | solution.py:400
  65.9 0.0 collective-permute-done.2.one_ref
  65.9 4.1 %apply.1 = f32[2,64,16384]{2,1,0:T(8,128)} custom-call(f32[64,64]{1,0:T(8,128)S(1)} %collective-permute-done.2.one_ref, f32[64,64]{1,0:T(8,128)S(1)} %collective-permute-done.3.two_ref, f32[64,64]{1,0:T(8,128)S(1)} %collective-permute-done.4.three_ref, f32[64,64]{1,0:T(8,128)S(1)} %fusion.first_ref, f32[64,64]{1,0:T(8,128)S(1)} %fusion.1.second_ref, ...), custom_call_target="tpu_custom_call" | custom-call | tf_op jit(solution)/shard_map/apply/pallas_call | solution.py:402
Async XLA Ops:
  2.1 21.3 %all-to-all-start = ((f32[32,3,4,128]{3,2,1,0:T(4,128)}), f32[32,3,4,128]{3,2,1,0:T(4,128)S(1)}, u32[]{:S(2)}, u32[]{:S(2)}) async-start(f32[32,3,4,128]{3,2,1,0:T(4,128)} %route.1), calls=%async_computation | async-start | bytes 393216 | tf_op jit(solution)/shard_map/all_to_all | solution.py:330
  13.9 31.1 %copy-start = (f32[2]{0:T(128)S(1)}, f32[2]{0:T(128)}, u32[]{:S(2)}) copy-start(f32[2]{0:T(128)} %param.15) | copy-start | bytes 28
  48.1 4.5 %collective-permute-start = (f32[64,64]{1,0:T(8,128)S(1)}, f32[64,64]{1,0:T(8,128)S(1)}, u32[]{:S(2)}, u32[]{:S(2)}) collective-permute-start(f32[64,64]{1,0:T(8,128)S(1)} %transform.1.made_ref.after_ref), channel_id=1, source_target_pairs={{0,1},{1,0},{2,3},{3,2},{4,5},{5,4},{6,7},{7,6},{8,9},{9,8},{10,11... | collective-permute-start | bytes 49160 | tf_op jit(solution)/shard_map/ppermute | solution.py:369
  52.8 5.9 %collective-permute-start.1 = (f32[64,64]{1,0:T(8,128)S(1)}, f32[64,64]{1,0:T(8,128)S(1)}, u32[]{:S(2)}, u32[]{:S(2)}) collective-permute-start(f32[64,64]{1,0:T(8,128)S(1)} %get-tuple-element.9.product_ref), channel_id=1, source_target_pairs={{0,32},{32,0},{64,96},{96,64},{128,160},{160,128},{192,224},{224,1... | collective-permute-start | bytes 49160 | tf_op jit(solution)/shard_map/ppermute | solution.py:389
  58.8 4.1 %collective-permute-start.4 = (f32[64,64]{1,0:T(8,128)S(1)}, f32[64,64]{1,0:T(8,128)S(1)}, u32[]{:S(2)}, u32[]{:S(2)}) collective-permute-start(f32[64,64]{1,0:T(8,128)S(1)} %get-tuple-element.10), channel_id=1, source_target_pairs={{0,192},{32,224},{64,128},{96,160},{128,64},{160,96},{192,0},{224,... | collective-permute-start | bytes 49160 | tf_op jit(solution)/shard_map/ppermute | solution.py:400
  61.6 4.3 %collective-permute-start.3 = (f32[64,64]{1,0:T(8,128)S(1)}, f32[64,64]{1,0:T(8,128)S(1)}, u32[]{:S(2)}, u32[]{:S(2)}) collective-permute-start(f32[64,64]{1,0:T(8,128)S(1)} %get-tuple-element.10), channel_id=1, source_target_pairs={{0,128},{32,160},{64,192},{96,224},{128,0},{160,32},{192,64},{224,... | collective-permute-start | bytes 49160 | tf_op jit(solution)/shard_map/ppermute | solution.py:400
  62.0 3.9 %collective-permute-start.2 = (f32[64,64]{1,0:T(8,128)S(1)}, f32[64,64]{1,0:T(8,128)S(1)}, u32[]{:S(2)}, u32[]{:S(2)}) collective-permute-start(f32[64,64]{1,0:T(8,128)S(1)} %get-tuple-element.10), channel_id=1, source_target_pairs={{0,64},{32,96},{64,0},{96,32},{128,192},{160,224},{192,128},{224,1... | collective-permute-start | bytes 49160 | tf_op jit(solution)/shard_map/ppermute | solution.py:400

commit v6 on v5

--- a/solution.py
+++ b/solution.py
@@ -192,6 +192,10 @@
         out_ref[d] = lines[d % 2]
 
 
+def spread(tile, place):
+    return jnp.take_along_axis(tile, jnp.full(tile.shape, place, jnp.int32), axis=1, mode="promise_in_bounds")
+
+
 def eliminate(systems):
     row, lane = iota((MEMB, 2 * MEMB), 0), iota((MEMB, 2 * MEMB), 1)
     eye = jnp.where(row + MEMB == lane, 1.0, 0.0)
@@ -206,8 +210,7 @@
         for w in range(count):
             rows = [jnp.broadcast_to(tiles[w][(j + k) // 8][(j + k) % 8][None], full) for k in range(STEP)]
             block = [
-                [jnp.broadcast_to(rows[k][:, j + l : j + l + 1], full) if l >= k else None for l in range(STEP)]
-                for k in range(STEP)
+                [spread(rows[k], j + l) if l >= k else None for l in range(STEP)] for k in range(STEP)
             ]
             inverses, lower = [], [[None] * STEP for _ in range(STEP)]
             for k in range(STEP):
@@ -224,17 +227,26 @@
             first = (j + STEP) // 8
             if first == MEMB // 8:
                 continue
+            tile = tiles[w][first]
+            columns = [spread(tile, j + k) for k in range(STEP)]
+            for k in range(STEP):
+                tile = tile - columns[k] * (rows[k] * inverses[k])
+                for l in range(k + 1, STEP):
+                    columns[l] = columns[l] - lower[l][k] * columns[k]
+            tiles[w][first] = tile
+            if first + 1 == MEMB // 8:
+                continue
             solved = [None] * STEP
             for k in reversed(range(STEP)):
                 value = rows[k] * inverses[k]
                 for l in range(k + 1, STEP):
                     value = value - lower[l][k] * solved[l]
                 solved[k] = value
-            for i in range(first, MEMB // 8):
+            for i in range(first + 1, MEMB // 8):
                 tile = tiles[w][i]
                 change = None
                 for k in range(STEP):
-                    part = jnp.broadcast_to(tile[:, j + k : j + k + 1], full) * solved[k]
+                    part = spread(tile, j + k) * solved[k]
                     change = part if change is None else change + part
                 tiles[w][i] = tile - change
     return [jnp.concatenate(rows, axis=0)[:, MEMB:] for rows in found]

time: 70.3 us -> 69.2 us (0.984)
  Pallas kernels: 20.8 us -> 19.8 us
    pallas_call x1, Pallas kernels: 3.12 us -> 2.06 us  [body(): pl.pallas_call(transform_kernel, out_shape=pltpu.VMEM((MEMB, MEMB), f32),...]
where the time goes in v6:
time: 69.2 us; the launch traced here: 68.9 us
  starting transfers between devices  22.1 us (32%)
  Pallas kernels  19.8 us (29%)
  blocking collectives  15 us (22%)
  waiting for transfers between devices  11.6 us (17%)
    all_to_all x1, blocking collectives, body(): lax.all_to_all(partial, 'space', split_axis=0, concat_axis=0, tiled=True)  15 us
    all_to_all x1, starting transfers between devices, body(): lax.all_to_all(routed, 'space', split_axis=0, concat_axis=0, tiled=True)  11.9 us
    all_to_all x1, waiting for transfers between devices, body(): lax.all_to_all(routed, 'space', split_axis=0, concat_axis=0, tiled=True)  7.03 us
    pallas_call x1, Pallas kernels, body(): pl.pallas_call(gram_kernel, out_shape=pltpu.VMEM((SHARDS, 2, LINE * 128),...  6.63 us
    pallas_call x1, Pallas kernels, body(): pl.pallas_call(apply_kernel, out_shape=jax.ShapeDtypeStruct((2, MEMB, CEL...  4.12 us
    ppermute x1, starting transfers between devices, body(): other = lax.ppermute(product, 'tm', [(i, i ^ 1) for i in range(8)])  3.6 us
    ppermute x3, starting transfers between devices, body(): lax.ppermute(joined, 'tm', [(i, i ^ bits) for i in range(8)])  3.49 us
    ppermute x3, waiting for transfers between devices, body(): lax.ppermute(joined, 'tm', [(i, i ^ bits) for i in range(8)])  3.26 us
  transfers between devices with their start and end apart: 6, of which 4 were waited for; matrix products, arithmetic and copies ran while one was open for 0% of the time, Pallas kernels for 7%

profile of v6, /device:TPU:1, one launch (start us, length us, event | category | flops | bytes accessed | tf_op | source)
XLA Modules:
  0.0 68.9 jit_solution(17760990716484617731)
XLA Ops:
  0.0 2.1 %route.1 = f32[32,3,4,128]{3,2,1,0:T(4,128)} custom-call(s32[2,128]{1,0:T(2,128)} %bitcast.13, s32[2,128]{1,0:T(2,128)} %local_ref.1, s32[2,32,128]{2,1,0:T(8,128)} %bitcast.10, s32[2,128]{1,0:T(2,128)} %count_ref.1, f32[2,32,128]{2,1,0:T(8,128)} %bitcast.11, f32[2,32,128]{2,1,0:T(8,128)} %bitcast.12), custom_call_target="tpu_custom_call" | custom-call | tf_op jit(solution)/shard_map/route/pallas_call | solution.py:335
  2.1 11.9 %all-to-all-start = ((f32[32,3,4,128]{3,2,1,0:T(4,128)}), f32[32,3,4,128]{3,2,1,0:T(4,128)S(1)}, u32[]{:S(2)}, u32[]{:S(2)}) async-start(f32[32,3,4,128]{3,2,1,0:T(4,128)} %route.1), calls=%async_computation | async-start | bytes 393216 | tf_op jit(solution)/shard_map/all_to_all | solution.py:342
  13.9 0.0 copy-start
  13.9 2.3 %center.1.mean_ref = f32[2,64,256]{2,1,0:T(8,128)S(1)} custom-call(bf16[2,64,16384]{2,1,0:T(8,128)(2,1)} %ens_hbm.5), custom_call_target="tpu_custom_call" | custom-call | tf_op jit(solution)/shard_map/center/pallas_call | solution.py:344
  16.3 7.0 %all-to-all-done.recv_ref = f32[32,3,4,128]{3,2,1,0:T(4,128)S(1)} async-done(((f32[32,3,4,128]{3,2,1,0:T(4,128)}), f32[32,3,4,128]{3,2,1,0:T(4,128)S(1)}, u32[]{:S(2)}, u32[]{:S(2)}) %all-to-all-start) | async-done | bytes 196640 | tf_op jit(solution)/shard_map/all_to_all | solution.py:342
  23.3 6.6 %gram.1 = f32[32,2,1152]{2,1,0:T(2,128)S(1)} custom-call(f32[32,3,4,128]{3,2,1,0:T(4,128)S(1)} %all-to-all-done.recv_ref, f32[2,64,256]{2,1,0:T(8,128)S(1)} %center.1.mean_ref, bf16[2,64,16384]{2,1,0:T(8,128)(2,1)} %ens_hbm.5), custom_call_target="tpu_custom_call" | custom-call | tf_op jit(solution)/shard_map/gram/pallas_call | solution.py:353
  30.0 15.0 %all_to_all.10.parts_ref = f32[32,2,1152]{2,1,0:T(2,128)S(1)} all-to-all(f32[32,2,1152]{2,1,0:T(2,128)S(1)} %gram.1), channel_id=1, replica_groups=mesh['tm'=8,'space'=32] {'space'}, dimensions={0} | all-to-all | bytes 589824 | tf_op jit(solution)/shard_map/all_to_all | solution.py:372
  45.0 0.0 copy-done
  45.0 2.1 %transform.1.made_ref.after_ref = f32[64,64]{1,0:T(8,128)S(1)} custom-call(f32[1,2]{1,0:T(1,128)S(1)} %bitcast.9, f32[32,2,1152]{2,1,0:T(2,128)S(1)} %all_to_all.10.parts_ref), custom_call_target="tpu_custom_call" | custom-call | tf_op jit(solution)/shard_map/transform/pallas_call | solution.py:373
  47.0 3.2 %collective-permute-start = (f32[64,64]{1,0:T(8,128)S(1)}, f32[64,64]{1,0:T(8,128)S(1)}, u32[]{:S(2)}, u32[]{:S(2)}) collective-permute-start(f32[64,64]{1,0:T(8,128)S(1)} %transform.1.made_ref.after_ref), channel_id=1, source_target_pairs={{0,1},{1,0},{2,3},{3,2},{4,5},{5,4},{6,7},{7,6},{8,9},{9,8},{10,11... | collective-permute-start | bytes 49160 | tf_op jit(solution)/shard_map/ppermute | solution.py:381
  50.2 1.3 %collective-permute-done.paired_ref = f32[64,64]{1,0:T(8,128)S(1)} collective-permute-done((f32[64,64]{1,0:T(8,128)S(1)}, f32[64,64]{1,0:T(8,128)S(1)}, u32[]{:S(2)}, u32[]{:S(2)}) %collective-permute-start) | collective-permute-done | bytes 16416 | tf_op jit(solution)/shard_map/ppermute | solution.py:381
  51.5 0.2 pair.1
  51.7 3.6 %collective-permute-start.1 = (f32[64,64]{1,0:T(8,128)S(1)}, f32[64,64]{1,0:T(8,128)S(1)}, u32[]{:S(2)}, u32[]{:S(2)}) collective-permute-start(f32[64,64]{1,0:T(8,128)S(1)} %get-tuple-element.9.product_ref), channel_id=1, source_target_pairs={{0,32},{32,0},{64,96},{96,64},{128,160},{160,128},{192,224},{224,1... | collective-permute-start | bytes 49160 | tf_op jit(solution)/shard_map/ppermute | solution.py:401
  55.3 2.2 %fetch.1.ens_ref = bf16[2,64,16384]{2,1,0:T(8,128)(2,1)S(1)} custom-call(f32[64,64]{1,0:T(8,128)S(1)} %transform.1.made_ref.after_ref, bf16[2,64,16384]{2,1,0:T(8,128)(2,1)} %ens_hbm.5), custom_call_target="tpu_custom_call" | custom-call | tf_op jit(solution)/shard_map/fetch/pallas_call | solution.py:382
  57.5 0.0 collective-permute-done.1.other_ref
  57.6 0.2 join.1
  57.7 2.8 %collective-permute-start.4 = (f32[64,64]{1,0:T(8,128)S(1)}, f32[64,64]{1,0:T(8,128)S(1)}, u32[]{:S(2)}, u32[]{:S(2)}) collective-permute-start(f32[64,64]{1,0:T(8,128)S(1)} %get-tuple-element.10), channel_id=1, source_target_pairs={{0,192},{32,224},{64,128},{96,160},{128,64},{160,96},{192,0},{224,... | collective-permute-start | bytes 49160 | tf_op jit(solution)/shard_map/ppermute | solution.py:412
  60.5 0.4 collective-permute-start.3
  60.9 0.3 collective-permute-start.2
  61.2 0.2 fusion.first_ref
  61.4 0.2 fusion.1.second_ref
  61.6 0.3 collective-permute-done.4.three_ref
  61.9 3.0 %collective-permute-done.3.two_ref = f32[64,64]{1,0:T(8,128)S(1)} collective-permute-done((f32[64,64]{1,0:T(8,128)S(1)}, f32[64,64]{1,0:T(8,128)S(1)}, u32[]{:S(2)}, u32[]{:S(2)}) %collective-permute-start.3) | collective-permute-done | bytes 16416 | tf_op jit(solution)/shard_map/ppermute | solution.py:412
  64.8 0.0 collective-permute-done.2.one_ref
  64.8 4.1 %apply.1 = f32[2,64,16384]{2,1,0:T(8,128)} custom-call(f32[64,64]{1,0:T(8,128)S(1)} %collective-permute-done.2.one_ref, f32[64,64]{1,0:T(8,128)S(1)} %collective-permute-done.3.two_ref, f32[64,64]{1,0:T(8,128)S(1)} %collective-permute-done.4.three_ref, f32[64,64]{1,0:T(8,128)S(1)} %fusion.first_ref, f32[64,64]{1,0:T(8,128)S(1)} %fusion.1.second_ref, ...), custom_call_target="tpu_custom_call" | custom-call | tf_op jit(solution)/shard_map/apply/pallas_call | solution.py:414
Async XLA Ops:
  2.1 21.3 %all-to-all-start = ((f32[32,3,4,128]{3,2,1,0:T(4,128)}), f32[32,3,4,128]{3,2,1,0:T(4,128)S(1)}, u32[]{:S(2)}, u32[]{:S(2)}) async-start(f32[32,3,4,128]{3,2,1,0:T(4,128)} %route.1), calls=%async_computation | async-start | bytes 393216 | tf_op jit(solution)/shard_map/all_to_all | solution.py:342
  13.9 31.1 %copy-start = (f32[2]{0:T(128)S(1)}, f32[2]{0:T(128)}, u32[]{:S(2)}) copy-start(f32[2]{0:T(128)} %param.15) | copy-start | bytes 28
  47.0 4.5 %collective-permute-start = (f32[64,64]{1,0:T(8,128)S(1)}, f32[64,64]{1,0:T(8,128)S(1)}, u32[]{:S(2)}, u32[]{:S(2)}) collective-permute-start(f32[64,64]{1,0:T(8,128)S(1)} %transform.1.made_ref.after_ref), channel_id=1, source_target_pairs={{0,1},{1,0},{2,3},{3,2},{4,5},{5,4},{6,7},{7,6},{8,9},{9,8},{10,11... | collective-permute-start | bytes 49160 | tf_op jit(solution)/shard_map/ppermute | solution.py:381
  51.7 5.9 %collective-permute-start.1 = (f32[64,64]{1,0:T(8,128)S(1)}, f32[64,64]{1,0:T(8,128)S(1)}, u32[]{:S(2)}, u32[]{:S(2)}) collective-permute-start(f32[64,64]{1,0:T(8,128)S(1)} %get-tuple-element.9.product_ref), channel_id=1, source_target_pairs={{0,32},{32,0},{64,96},{96,64},{128,160},{160,128},{192,224},{224,1... | collective-permute-start | bytes 49160 | tf_op jit(solution)/shard_map/ppermute | solution.py:401
  57.7 4.1 %collective-permute-start.4 = (f32[64,64]{1,0:T(8,128)S(1)}, f32[64,64]{1,0:T(8,128)S(1)}, u32[]{:S(2)}, u32[]{:S(2)}) collective-permute-start(f32[64,64]{1,0:T(8,128)S(1)} %get-tuple-element.10), channel_id=1, source_target_pairs={{0,192},{32,224},{64,128},{96,160},{128,64},{160,96},{192,0},{224,... | collective-permute-start | bytes 49160 | tf_op jit(solution)/shard_map/ppermute | solution.py:412
  60.5 4.3 %collective-permute-start.3 = (f32[64,64]{1,0:T(8,128)S(1)}, f32[64,64]{1,0:T(8,128)S(1)}, u32[]{:S(2)}, u32[]{:S(2)}) collective-permute-start(f32[64,64]{1,0:T(8,128)S(1)} %get-tuple-element.10), channel_id=1, source_target_pairs={{0,128},{32,160},{64,192},{96,224},{128,0},{160,32},{192,64},{224,... | collective-permute-start | bytes 49160 | tf_op jit(solution)/shard_map/ppermute | solution.py:412
  60.9 3.9 %collective-permute-start.2 = (f32[64,64]{1,0:T(8,128)S(1)}, f32[64,64]{1,0:T(8,128)S(1)}, u32[]{:S(2)}, u32[]{:S(2)}) collective-permute-start(f32[64,64]{1,0:T(8,128)S(1)} %get-tuple-element.10), channel_id=1, source_target_pairs={{0,64},{32,96},{64,0},{96,32},{128,192},{160,224},{192,128},{224,1... | collective-permute-start | bytes 49160 | tf_op jit(solution)/shard_map/ppermute | solution.py:412
